TPU v7x, 32 devices: a whole 2x2x4 slice. The times are simulated.
32 devices in a mesh: groups: 2 (over x), vid: 8 (over z, y), tok: 2 (over core).
Axes of the slice: x: 2, y: 2, z: 4, core: 2. Of those that a mesh axis runs over, the one named last changes fastest.
Arguments:
- captions: bfloat16 [16, 128, 32, 128], P(('groups', 'vid')), parts along dimension 0, may hold values from -8 to 8
- caption_lengths: int32 [16, 128], P(('groups', 'vid')), parts along dimension 0, may hold values from 1 to 32
- video_bank: bfloat16 [192, 256, 128], P(('groups', 'vid'), 'tok'), parts along dimension 0, may hold values from -1.5 to 1.5
- owner_order: int32 [6], P('groups'), parts along dimension 0, may hold values from 0 to 7, as said below
Outputs:
- scores: float32 [192, 384], P(('groups', 'vid')), parts along dimension 0
There are 2 independent parts, one for each index of `groups`. A program takes and returns all parts, laid end to end along the dimension named above; each array names one. Nothing has to cross between parts.
Inputs may be any that keep to these rules, and one draw needn't show every extreme that they name: `caption_lengths`: token slot j of a caption is real when j is less than its count. `owner_order`: 3 different block indices.
All inputs are finite; a program needn't handle non-finite values.
Results may differ from a plain program's by a relative error of at most 0.0003.
Values may be sent and summed in bfloat16 or wider, within the bound.
No kernel may reach another device: no remote copies, remote signals or barrier semaphores. Data moves between devices by JAX's collectives and lax.ppermute only.
A program may use at most 64 MiB of HBM per device.

v0:
```python
import functools

import jax
import jax.numpy as jnp
from jax import lax
from jax.experimental import pallas as pl
from jax.experimental.pallas import tpu as pltpu
from jax.sharding import PartitionSpec as P


SHARPNESS = 5.0
LOG2E = 1.4426950408889634
LN2 = 0.6931471805599453
COUNT_ROWS = 8
PAIR = 2
STEPS = 4
TILE = 256
LANES = 128
FIRST_JOB = 2
LEAST = 2.0**-90
MOST = 2.0**120
VMEM_BYTES = 24 << 20
F32 = jnp.float32
BF16 = jnp.bfloat16


def dot(a, b, dims):
    return lax.dot_general(a, b, (dims, ((), ())), preferred_element_type=F32)


def thirds(x):
    parts = []
    for _ in range(3):
        parts.append(x.astype(BF16))
        x = x - parts[-1].astype(F32)
    return parts


def score_kernel(slots, caps, share, last, meta_ref, lanes_ref, q_ref, bank_ref, *refs):
    past, refs = (refs[:1], refs[1:]) if share else ((), refs)
    outs, refs = refs[: 1 + last], refs[1 + last :]
    out_ref, (rows_ref, soft_ref, bad_ref, a_ref, b_ref) = refs[0] if last else outs[0], refs[last:]
    blocks, rounds = q_ref.shape[:2]
    videos, tokens = bank_ref.shape[0] // 2, bank_ref.shape[1]
    total_rows = meta_ref[3, share]

    def pack(i, carry):
        r, g = i // blocks, i % blocks
        piece = q_ref[g, r].astype(F32)
        for c in range(caps):
            start = meta_ref[0, (share * rounds * blocks + i) * caps + c]
            rows_ref[pl.ds(start, slots), :] = piece[c * slots : (c + 1) * slots]
        return carry

    lax.fori_loop(0, rounds * blocks, pack, 0)
    lane = lax.broadcasted_iota(jnp.int32, (1, LANES), 1)
    here = lane // (rounds * blocks * caps) == share
    first = lanes_ref[0:1, :]
    end = jnp.where(here, first + lanes_ref[1:2, :], 0)
    scale = F32(SHARPNESS * LOG2E)
    jobs = [(0, FIRST_JOB), (FIRST_JOB, 2 * videos - FIRST_JOB)]
    bufs = (a_ref, b_ref)

    def products(dst, job, w):
        first, size = job
        bank = bank_ref[first : first + size].reshape(size * tokens, bank_ref.shape[2])
        dst[...] = dot(jnp.concatenate([bank, bank], axis=1), w, ((1,), (1,)))

    def unit(src, v, col, shifted):
        x = src[v * tokens : (v + 1) * tokens, col : col + LANES].reshape(tokens // 8, 8, LANES)
        if not shifted:
            return None, jnp.sum(jnp.sum(jnp.exp2(x), axis=0), axis=0, keepdims=True)
        top = jnp.max(x, axis=0)
        total = jnp.sum(jnp.exp2(x - top[None]), axis=0)
        peak = jnp.max(top, axis=0, keepdims=True)
        return peak, jnp.sum(total * jnp.exp2(top - peak), axis=0, keepdims=True)

    def weights(i):
        q = rows_ref[pl.ds(pl.multiple_of(i * TILE, TILE), TILE), :] * scale
        high = q.astype(BF16)
        return jnp.concatenate([high, (q - high.astype(F32)).astype(BF16)], axis=1)

    def collect(i, shifted):
        sums = soft_ref[1]
        soft = jnp.log2(sums)
        if shifted:
            soft = soft + soft_ref[0]
        col = i * TILE + lax.broadcasted_iota(jnp.int32, soft.shape, 1)
        valid = (col >= 0) & (col < total_rows)
        if not shifted:
            fine = (sums > LEAST) & (sums < MOST)
            bad_ref[...] = jnp.where(valid & ~fine, 1.0, bad_ref[...])
        soft = jnp.where(valid, soft * F32(LN2 / SHARPNESS), 0.0)
        parts = jnp.concatenate(thirds(soft), axis=0)
        row = i * TILE + lax.broadcasted_iota(jnp.int32, (TILE, LANES), 0)
        n = 2 * videos
        member = jnp.where((row >= first) & (row < end), F32(1), F32(0))
        got = dot(parts, member.astype(BF16), ((1,), (0,)))
        out_ref[...] += got[:n] + got[n : 2 * n] + got[2 * n :]

    def tile(shifted, i, carry):
        w = weights(i)
        collect(i - 1, shifted)
        for j, (base, size) in enumerate(jobs):
            after = (jobs[j + 1], w) if j + 1 < len(jobs) else (jobs[0], weights(i + 1))
            products(bufs[(j + 1) % 2], *after)
            for v in range(size):
                for col in range(0, TILE, LANES):
                    peak, total = unit(bufs[j % 2], v, col, shifted)
                    at = base + v
                    if shifted:
                        soft_ref[0, at : at + 1, col : col + LANES] = peak
                    soft_ref[1, at : at + 1, col : col + LANES] = total
        return carry

    tiles = (total_rows + TILE - 1) // TILE

    def run(shifted):
        out_ref[...] = past[0][...] if past else jnp.zeros_like(out_ref)
        products(bufs[0], jobs[0], weights(0))
        lax.fori_loop(0, tiles, functools.partial(tile, shifted), 0)
        collect(tiles - 1, shifted)

    bad_ref[...] = jnp.zeros_like(bad_ref)
    run(False)

    @pl.when(jnp.max(bad_ref[...]) > 0)
    def _():
        run(True)

    if last:
        mean = out_ref[...] / jnp.maximum(lanes_ref[1:2, :], 1).astype(F32)
        column = lax.broadcasted_iota(jnp.int32, (rounds * LANES, LANES), 0)
        spread = jnp.where(column == lanes_ref[2:3, :], F32(1), F32(0)).astype(BF16)
        n = 2 * videos
        got = dot(jnp.concatenate(thirds(mean), axis=0), spread, ((1,), (1,)))
        got = got[:n] + got[n : 2 * n] + got[2 * n :]
        outs[0][...] = got[:videos]
        outs[1][...] = got[videos:]


def share_scores(slots, caps, share, last, meta, query, bank, *past):
    blocks, rounds, rows, width = query.shape
    videos, tokens = bank.shape[0] // 2, bank.shape[1]
    n_rows = -(-(rounds * blocks * rows) // TILE) * TILE + TILE + slots
    vmem = pl.BlockSpec(memory_space=pltpu.VMEM)
    work = 2 * videos * tokens * rounds * blocks * rows
    total = (2 * videos, LANES)
    outs = [(videos, rounds * LANES)] * 2 if last else [total]
    return pl.pallas_call(
        lambda *refs: score_kernel(slots, caps, share, last, *refs),
        in_specs=[pl.BlockSpec(memory_space=pltpu.SMEM)] + [vmem] * (3 + len(past)),
        out_specs=[vmem] * len(outs),
        out_shape=[jax.ShapeDtypeStruct(shape, F32) for shape in outs],
        scratch_shapes=[pltpu.VMEM(total, F32)] * last
        + [
            pltpu.VMEM((n_rows, width), F32),
            pltpu.VMEM((2, 2 * videos, TILE), F32),
            pltpu.VMEM((2 * videos, TILE), F32),
            pltpu.VMEM((FIRST_JOB * tokens, TILE), F32),
            pltpu.VMEM(((2 * videos - FIRST_JOB) * tokens, TILE), F32),
        ],
        compiler_params=pltpu.CompilerParams(vmem_limit_bytes=VMEM_BYTES),
        cost_estimate=pl.CostEstimate(
            flops=4 * work * width, transcendentals=work, bytes_accessed=bank.size * 2
        ),
        name="soft_scores",
    )(meta, meta, query, bank, *past)


def merge_kernel(caps, blocks, inner, quarters, vid_axis, tok_axis, order_ref, own_ref, tok_ref,
                 pair_ref, both_ref, counts_ref, bank_ref, meta_ref, sems):
    videos, half = own_ref.shape[:2]
    rounds = order_ref.shape[0]
    moves = []
    for k, src in enumerate((own_ref, tok_ref, pair_ref, both_ref)):
        dst = bank_ref.at[pl.ds(k // 2 * videos, videos), pl.ds(k % 2 * half, half), :]
        moves.append(pltpu.make_async_copy(src, dst, sems.at[k]))
        moves[-1].start()
    vid = lax.axis_index(vid_axis)
    quarter = vid % PAIR * (quarters // PAIR) + lax.axis_index(tok_axis)
    place = vid // PAIR % inner
    per = rounds * blocks * caps

    def where(lane):
        share, rest = lane // per, lane % per
        block = rest // caps % blocks * inner + (share ^ place)
        return share, rest // (blocks * caps), (block * quarters + quarter) * caps + lane % caps

    down = lax.broadcasted_iota(jnp.int32, (LANES, LANES), 0)
    across = lax.broadcasted_iota(jnp.int32, (LANES, LANES), 1)
    share, turn, cap = where(lax.broadcasted_iota(jnp.int32, (1, LANES), 1))
    used = share < inner
    counts = jnp.zeros((COUNT_ROWS, LANES), F32)
    for r in range(rounds):
        pick = jnp.where((down == cap) & (turn == r) & used, F32(1), F32(0)).astype(BF16)
        counts = counts + dot(counts_ref[r], pick, ((1,), (0,)))
    before = jnp.where((down < across) & (down // per == share), F32(1), F32(0)).astype(BF16)
    within = jnp.where(down // per == across, F32(1), F32(0)).astype(BF16)
    starts = dot(counts.astype(BF16), before, ((1,), (0,)))
    totals = dot(counts.astype(BF16), within, ((1,), (0,)))
    meta_ref[...] = jnp.zeros_like(meta_ref)
    meta_ref[0:1, :] = starts[:1].astype(jnp.int32)
    meta_ref[1:2, :] = counts[:1].astype(jnp.int32)
    meta_ref[2:3, :] = jnp.where(used, turn * LANES + cap, -1)
    meta_ref[3:4, :] = totals[:1].astype(jnp.int32)
    for move in moves:
        move.wait()


def prepare_kernel(tok_axis, block_ref, counts_ref, out_ref, piece_ref, count_ref, in_sems, out_sems):
    n, rows = block_ref.shape[0], block_ref.shape[2]
    tok = lax.axis_index(tok_axis)
    lengths = pltpu.make_async_copy(counts_ref, count_ref, in_sems.at[n])
    lengths.start()
    moves = []
    for k in range(n):
        moves.append(
            pltpu.make_async_copy(block_ref.at[k, tok], piece_ref.at[k, pl.ds(0, rows)], in_sems.at[k])
        )
        moves[-1].start()
    lengths.wait()
    counts = jnp.broadcast_to(count_ref[...], (COUNT_ROWS, LANES)).astype(F32).astype(BF16)
    for k in range(n):
        piece_ref[k, rows:, :] = counts
    for k in range(n):
        moves[k].wait()
        moves[k] = pltpu.make_async_copy(piece_ref.at[k], out_ref.at[k], out_sems.at[k])
        moves[k].start()
    for move in moves:
        move.wait()


def pick_kernel(order_ref, shares_ref, wanted_ref, counts_ref):
    rows = shares_ref.shape[1] - COUNT_ROWS
    for r in range(order_ref.shape[0]):
        owner = order_ref[r]
        wanted_ref[r * rows : (r + 1) * rows, :] = shares_ref[owner, :rows, :]
        counts_ref[r] = shares_ref[owner, rows:, :]


def per_device(captions, caption_lengths, video_bank, owner_order):
    n_vid, n_tok = lax.axis_size("vid"), lax.axis_size("tok")
    capb, slots, width = captions.shape[1:]
    rounds = owner_order.shape[0]
    videos, half = video_bank.shape[:2]
    line = n_vid // PAIR
    caps = capb // (n_vid * n_tok)
    rows = caps * slots
    swap_tok = [(0, 1), (1, 0)]
    swap_pair = [(i, i ^ 1) for i in range(n_vid)]
    swap_both = [
        (i * n_tok + t, (i ^ 1) * n_tok + (t ^ 1)) for i in range(n_vid) for t in range(n_tok)
    ]
    vmem = pl.BlockSpec(memory_space=pltpu.VMEM)
    small = pltpu.CompilerParams(vmem_limit_bytes=VMEM_BYTES)

    tok_bank = lax.ppermute(video_bank, "tok", swap_tok)
    pair_bank = lax.ppermute(video_bank, "vid", swap_pair)

    pieces = pl.pallas_call(
        lambda *refs: prepare_kernel("tok", *refs),
        in_specs=[pl.BlockSpec(memory_space=pltpu.HBM)] * 2,
        out_specs=pl.BlockSpec(memory_space=pltpu.HBM),
        out_shape=jax.ShapeDtypeStruct((n_vid, rows + COUNT_ROWS, width), captions.dtype),
        scratch_shapes=[
            pltpu.VMEM((n_vid, rows + COUNT_ROWS, width), captions.dtype),
            pltpu.VMEM(caption_lengths.shape, caption_lengths.dtype),
            pltpu.SemaphoreType.DMA((n_vid + 1,)),
            pltpu.SemaphoreType.DMA((n_vid,)),
        ],
        name="prepare",
    )(captions.reshape(n_vid, n_tok, rows, width), caption_lengths)
    shares = lax.all_to_all(pieces, "vid", 0, 0, tiled=True)
    wanted, counts = pl.pallas_call(
        pick_kernel,
        in_specs=[pl.BlockSpec(memory_space=pltpu.SMEM), vmem],
        out_specs=[vmem] * 2,
        out_shape=[
            jax.ShapeDtypeStruct((rounds * rows, width), captions.dtype),
            jax.ShapeDtypeStruct((rounds, COUNT_ROWS, width), captions.dtype),
        ],
        compiler_params=small,
        name="pick",
    )(owner_order, shares)
    inner = min(STEPS, line)
    blocks = line // inner
    if blocks > 1:
        groups = [
            [(b * inner + m) * PAIR + s for b in range(blocks)] for m in range(inner) for s in range(PAIR)
        ]
        wanted = lax.all_gather(wanted, "vid", axis=0, axis_index_groups=groups)
    wanted = wanted.reshape(blocks, rounds, rows, width)
    arrived = [wanted]
    for k in range(1, inner):
        steps = [(i, i ^ (k * PAIR)) for i in range(n_vid)]
        arrived.append(lax.ppermute(wanted, "vid", steps))

    both_bank = lax.ppermute(pair_bank, "tok", swap_tok)
    bank, meta = pl.pallas_call(
        lambda *refs: merge_kernel(caps, blocks, inner, PAIR * n_tok, "vid", "tok", *refs),
        in_specs=[pl.BlockSpec(memory_space=pltpu.SMEM)]
        + [pl.BlockSpec(memory_space=pl.ANY)] * 4
        + [vmem],
        out_specs=[vmem] * 2,
        out_shape=[
            jax.ShapeDtypeStruct((2 * videos, 2 * half, width), video_bank.dtype),
            jax.ShapeDtypeStruct((8, LANES), jnp.int32),
        ],
        scratch_shapes=[pltpu.SemaphoreType.DMA((4,))],
        compiler_params=small,
        name="merge",
    )(owner_order, video_bank, tok_bank, pair_bank, both_bank, counts)
    total = ()
    for k, query in enumerate(arrived):
        total = share_scores(slots, caps, k, k == inner - 1, meta, query, bank, *total)
    near, far = total
    near = near + lax.ppermute(near, "tok", swap_tok)
    return near + lax.ppermute(far, "vid", swap_pair) + lax.ppermute(far, ("vid", "tok"), swap_both)


def solution(mesh):
    return jax.shard_map(
        per_device,
        mesh=mesh,
        in_specs=(
            P(("groups", "vid"), None, None, None),
            P(("groups", "vid"), None),
            P(("groups", "vid"), "tok", None),
            P("groups"),
        ),
        out_specs=P(("groups", "vid"), None),
        check_vma=False,
    )
```

profile of v0, /device:TPU:11, one launch (start us, length us, event | category | flops | bytes accessed | tf_op | source)
XLA Modules:
  0.0 60.8 jit_solution(4406681440043239738)
XLA Ops:
  0.0 0.0 copy-start
  0.0 0.0 copy-start.1
  0.0 1.9 %prepare.1 = bf16[8,264,128]{2,1,0:T(8,128)(2,1)} custom-call(bf16[8,2,256,128]{3,2,1,0:T(8,128)(2,1)} %bitcast.6, s32[1,128]{1,0:T(1,128)} %refs_1_.2), custom_call_target="tpu_custom_call" | custom-call | tf_op jit(solution)/shard_map/prepare/pallas_call | solution.py:261
  1.9 5.7 %all-to-all-start = ((bf16[8,264,128]{2,1,0:T(8,128)(2,1)}), bf16[8,264,128]{2,1,0:T(8,128)(2,1)S(1)}, u32[]{:S(2)}, u32[]{:S(2)}) async-start(bf16[8,264,128]{2,1,0:T(8,128)(2,1)} %prepare.1), calls=%async_computation | async-start | bytes 1081344 | tf_op jit(solution)/shard_map/all_to_all | solution.py:274
  7.6 0.0 copy-done
  7.6 1.2 %collective-permute-start.1 = (bf16[12,128,128]{2,1,0:T(8,128)(2,1)S(1)}, bf16[12,128,128]{2,1,0:T(8,128)(2,1)S(1)}, u32[]{:S(2)}, u32[]{:S(2)}) collective-permute-start(bf16[12,128,128]{2,1,0:T(8,128)(2,1)S(1)} %copy-done), channel_id=1, source_target_pairs={{0,2},{2,0},{4,6},{6,4},{8,10},{10,8},{12,14},{14,12},{1,3},{3,1},... | collective-permute-start | bytes 1179656 | tf_op jit(solution)/shard_map/ppermute | solution.py:259
  8.8 1.5 %collective-permute-start = (bf16[12,128,128]{2,1,0:T(8,128)(2,1)S(1)}, bf16[12,128,128]{2,1,0:T(8,128)(2,1)S(1)}, u32[]{:S(2)}, u32[]{:S(2)}) collective-permute-start(bf16[12,128,128]{2,1,0:T(8,128)(2,1)S(1)} %copy-done), channel_id=1, source_target_pairs={{0,1},{1,0},{2,3},{3,2},{4,5},{5,4},{6,7},{7,6},{8,9},{9,8},{10,11... | collective-permute-start | bytes 1179656 | tf_op jit(solution)/shard_map/ppermute | solution.py:258
  10.3 12.7 %collective-permute-done.1.refs_3_ = bf16[12,128,128]{2,1,0:T(8,128)(2,1)S(1)} collective-permute-done((bf16[12,128,128]{2,1,0:T(8,128)(2,1)S(1)}, bf16[12,128,128]{2,1,0:T(8,128)(2,1)S(1)}, u32[]{:S(2)}, u32[]{:S(2)}) %collective-permute-start.1) | collective-permute-done | bytes 393248 | tf_op jit(solution)/shard_map/ppermute | solution.py:259
  23.1 1.8 %collective-permute-start.2 = (bf16[12,128,128]{2,1,0:T(8,128)(2,1)S(1)}, bf16[12,128,128]{2,1,0:T(8,128)(2,1)S(1)}, u32[]{:S(2)}, u32[]{:S(2)}) collective-permute-start(bf16[12,128,128]{2,1,0:T(8,128)(2,1)S(1)} %collective-permute-done.1.refs_3_), channel_id=1, source_target_pairs={{0,1},{1,0},{2,3},{3,2},{4,5},{5,4},{6,7},{7,6},{8,9},{9,8},{10,11... | collective-permute-start | bytes 1179656 | tf_op jit(solution)/shard_map/ppermute | solution.py:299
  24.9 0.0 all-to-all-done.shares_ref
  24.9 0.0 copy-done.1
  24.9 0.6 pick.1
  25.5 0.3 collective-permute-start.5
  25.8 2.1 %collective-permute-start.4 = (bf16[1,3,256,128]{3,2,1,0:T(8,128)(2,1)S(1)}, bf16[1,3,256,128]{3,2,1,0:T(8,128)(2,1)S(1)}, u32[]{:S(2)}, u32[]{:S(2)}) collective-permute-start(bf16[1,3,256,128]{3,2,1,0:T(8,128)(2,1)S(1)} %bitcast.3), channel_id=1, source_target_pairs={{0,8},{2,10},{4,12},{6,14},{8,0},{10,2},{12,4},{14,6},{1,9},{3,11}... | collective-permute-start | bytes 589832 | tf_op jit(solution)/shard_map/ppermute | solution.py:297
  27.9 0.3 collective-permute-start.3
  28.2 0.0 collective-permute-done.refs_2_
  28.2 0.0 collective-permute-done.2.refs_4_
  28.2 1.0 %merge.1 = (bf16[24,256,128]{2,1,0:T(8,128)(2,1)S(1)}, s32[8,128]{1,0:T(8,128)S(1)}) custom-call(s32[3]{0:T(128)S(1)} %copy-done.1, bf16[12,128,128]{2,1,0:T(8,128)(2,1)S(1)} %copy-done, bf16[12,128,128]{2,1,0:T(8,128)(2,1)S(1)} %collective-permute-done.refs_2_, bf16[12,128,128]{2,1,0:T(8,128)(2,1)S(1)} %collective-permute-done.1.refs_3_, ...), custom_call_target="tpu_custom_call" | custom-call | tf_op jit(solution)/shard_map/merge/pallas_call | solution.py:300
  29.2 6.6 %soft_scores.4.refs_4_ = f32[24,128]{1,0:T(8,128)S(1)} custom-call(s32[8,128]{1,0:T(8,128)S(1)} %get-tuple-element.12.refs_0_.refs_1_, s32[8,128]{1,0:T(8,128)S(1)} %get-tuple-element.12.refs_0_.refs_1_, bf16[1,3,256,128]{3,2,1,0:T(8,128)(2,1)S(1)} %bitcast.5, bf16[24,256,128]{2,1,0:T(8,128)(2,1)S(1)} %get-tuple-element.14.refs_3_), custom_call_target="tpu_custom_call" | custom-call | flops 2415919104 | bytes 1572864 | tf_op jit(solution)/shard_map/soft_scores/pallas_call | solution.py:150
  35.8 0.0 collective-permute-done.5.refs_2_
  35.8 3.2 %soft_scores.5.refs_4_ = f32[24,128]{1,0:T(8,128)S(1)} custom-call(s32[8,128]{1,0:T(8,128)S(1)} %get-tuple-element.12.refs_0_.refs_1_, s32[8,128]{1,0:T(8,128)S(1)} %get-tuple-element.12.refs_0_.refs_1_, bf16[1,3,256,128]{3,2,1,0:T(8,128)(2,1)S(1)} %collective-permute-done.5.refs_2_, bf16[24,256,128]{2,1,0:T(8,128)(2,1)S(1)} %get-tuple-element.14.refs_3_, ...), custom_call_target="tpu_custom_call" | custom-call | flops 2415919104 | bytes 1572864 | tf_op jit(solution)/shard_map/soft_scores/pallas_call | solution.py:150
  39.0 1.1 %collective-permute-done.4.refs_2_ = bf16[1,3,256,128]{3,2,1,0:T(8,128)(2,1)S(1)} collective-permute-done((bf16[1,3,256,128]{3,2,1,0:T(8,128)(2,1)S(1)}, bf16[1,3,256,128]{3,2,1,0:T(8,128)(2,1)S(1)}, u32[]{:S(2)}, u32[]{:S(2)}) %collective-permute-start.4) | collective-permute-done | bytes 196640 | tf_op jit(solution)/shard_map/ppermute | solution.py:297
  40.2 3.2 %soft_scores.6.refs_4_ = f32[24,128]{1,0:T(8,128)S(1)} custom-call(s32[8,128]{1,0:T(8,128)S(1)} %get-tuple-element.12.refs_0_.refs_1_, s32[8,128]{1,0:T(8,128)S(1)} %get-tuple-element.12.refs_0_.refs_1_, bf16[1,3,256,128]{3,2,1,0:T(8,128)(2,1)S(1)} %collective-permute-done.4.refs_2_, bf16[24,256,128]{2,1,0:T(8,128)(2,1)S(1)} %get-tuple-element.14.refs_3_, ...), custom_call_target="tpu_custom_call" | custom-call | flops 2415919104 | bytes 1572864 | tf_op jit(solution)/shard_map/soft_scores/pallas_call | solution.py:150
  43.4 2.2 %collective-permute-done.3.refs_2_ = bf16[1,3,256,128]{3,2,1,0:T(8,128)(2,1)S(1)} collective-permute-done((bf16[1,3,256,128]{3,2,1,0:T(8,128)(2,1)S(1)}, bf16[1,3,256,128]{3,2,1,0:T(8,128)(2,1)S(1)}, u32[]{:S(2)}, u32[]{:S(2)}) %collective-permute-start.3) | collective-permute-done | bytes 196640 | tf_op jit(solution)/shard_map/ppermute | solution.py:297
  45.6 3.4 %soft_scores.7 = (f32[12,384]{1,0:T(8,128)S(1)}, f32[12,384]{1,0:T(8,128)S(1)}) custom-call(s32[8,128]{1,0:T(8,128)S(1)} %get-tuple-element.12.refs_0_.refs_1_, s32[8,128]{1,0:T(8,128)S(1)} %get-tuple-element.12.refs_0_.refs_1_, bf16[1,3,256,128]{3,2,1,0:T(8,128)(2,1)S(1)} %collective-permute-done.3.refs_2_, ...), custom_call_target="tpu_custom_call" | custom-call | flops 2415919104 | bytes 1572864 | tf_op jit(solution)/shard_map/soft_scores/pallas_call | solution.py:150
  48.9 1.2 %collective-permute-start.6 = (f32[12,384]{1,0:T(8,128)S(1)}, f32[12,384]{1,0:T(8,128)S(1)}, u32[]{:S(2)}, u32[]{:S(2)}) collective-permute-start(f32[12,384]{1,0:T(8,128)S(1)} %get-tuple-element.15), channel_id=1, source_target_pairs={{0,1},{1,0},{2,3},{3,2},{4,5},{5,4},{6,7},{7,6},{8,9},{9,8},{10,11... | collective-permute-start | bytes 55304 | tf_op jit(solution)/shard_map/ppermute | solution.py:318
  50.1 6.2 %collective-permute-start.7 = (f32[12,384]{1,0:T(8,128)S(1)}, f32[12,384]{1,0:T(8,128)S(1)}, u32[]{:S(2)}, u32[]{:S(2)}) collective-permute-start(f32[12,384]{1,0:T(8,128)S(1)} %get-tuple-element.16), channel_id=1, source_target_pairs={{0,2},{2,0},{4,6},{6,4},{8,10},{10,8},{12,14},{14,12},{1,3},{3,1},... | collective-permute-start | bytes 55304 | tf_op jit(solution)/shard_map/ppermute | solution.py:319
  56.4 0.3 collective-permute-start.8
  56.7 0.0 collective-permute-done.6
  56.7 0.9 %collective-permute-done.7 = f32[12,384]{1,0:T(8,128)S(1)} collective-permute-done((f32[12,384]{1,0:T(8,128)S(1)}, f32[12,384]{1,0:T(8,128)S(1)}, u32[]{:S(2)}, u32[]{:S(2)}) %collective-permute-start.7) | collective-permute-done | bytes 18464 | tf_op jit(solution)/shard_map/ppermute | solution.py:319
  57.6 2.6 %collective-permute-done.8 = f32[12,384]{1,0:T(8,128)S(1)} collective-permute-done((f32[12,384]{1,0:T(8,128)S(1)}, f32[12,384]{1,0:T(8,128)S(1)}, u32[]{:S(2)}, u32[]{:S(2)}) %collective-permute-start.8) | collective-permute-done | bytes 18464 | tf_op jit(solution)/shard_map/ppermute | solution.py:319
  60.2 0.6 %add_add_fusion = f32[12,384]{1,0:T(8,128)} fusion(f32[12,384]{1,0:T(8,128)S(1)} %collective-permute-done.8, f32[12,384]{1,0:T(8,128)S(1)} %collective-permute-done.7, f32[12,384]{1,0:T(8,128)S(1)} %get-tuple-element.15, f32[12,384]{1,0:T(8,128)S(1)} %collective-permute-done.6), kind=kLoop, calls=%fused_computation | loop fusion | flops 13824 | bytes 92160 | tf_op jit(solution)/shard_map/add | solution.py:319
Async XLA Ops:
  0.0 7.6 %copy-start = (bf16[12,128,128]{2,1,0:T(8,128)(2,1)S(1)}, bf16[12,128,128]{2,1,0:T(8,128)(2,1)}, u32[]{:S(2)}) copy-start(bf16[12,128,128]{2,1,0:T(8,128)(2,1)} %refs_1_.3) | copy-start | bytes 1179652
  0.0 24.9 %copy-start.1 = (s32[3]{0:T(128)S(1)}, s32[3]{0:T(128)}, u32[]{:S(2)}) copy-start(s32[3]{0:T(128)} %refs_0_.1) | copy-start | bytes 40
  1.9 23.0 %all-to-all-start = ((bf16[8,264,128]{2,1,0:T(8,128)(2,1)}), bf16[8,264,128]{2,1,0:T(8,128)(2,1)S(1)}, u32[]{:S(2)}, u32[]{:S(2)}) async-start(bf16[8,264,128]{2,1,0:T(8,128)(2,1)} %prepare.1), calls=%async_computation | async-start | bytes 1081344 | tf_op jit(solution)/shard_map/all_to_all | solution.py:274
  7.6 15.4 %collective-permute-start.1 = (bf16[12,128,128]{2,1,0:T(8,128)(2,1)S(1)}, bf16[12,128,128]{2,1,0:T(8,128)(2,1)S(1)}, u32[]{:S(2)}, u32[]{:S(2)}) collective-permute-start(bf16[12,128,128]{2,1,0:T(8,128)(2,1)S(1)} %copy-done), channel_id=1, source_target_pairs={{0,2},{2,0},{4,6},{6,4},{8,10},{10,8},{12,14},{14,12},{1,3},{3,1},... | collective-permute-start | bytes 1179656 | tf_op jit(solution)/shard_map/ppermute | solution.py:259
  8.8 19.4 %collective-permute-start = (bf16[12,128,128]{2,1,0:T(8,128)(2,1)S(1)}, bf16[12,128,128]{2,1,0:T(8,128)(2,1)S(1)}, u32[]{:S(2)}, u32[]{:S(2)}) collective-permute-start(bf16[12,128,128]{2,1,0:T(8,128)(2,1)S(1)} %copy-done), channel_id=1, source_target_pairs={{0,1},{1,0},{2,3},{3,2},{4,5},{5,4},{6,7},{7,6},{8,9},{9,8},{10,11... | collective-permute-start | bytes 1179656 | tf_op jit(solution)/shard_map/ppermute | solution.py:258
  23.1 5.1 %collective-permute-start.2 = (bf16[12,128,128]{2,1,0:T(8,128)(2,1)S(1)}, bf16[12,128,128]{2,1,0:T(8,128)(2,1)S(1)}, u32[]{:S(2)}, u32[]{:S(2)}) collective-permute-start(bf16[12,128,128]{2,1,0:T(8,128)(2,1)S(1)} %collective-permute-done.1.refs_3_), channel_id=1, source_target_pairs={{0,1},{1,0},{2,3},{3,2},{4,5},{5,4},{6,7},{7,6},{8,9},{9,8},{10,11... | collective-permute-start | bytes 1179656 | tf_op jit(solution)/shard_map/ppermute | solution.py:299
  25.5 10.4 %collective-permute-start.5 = (bf16[1,3,256,128]{3,2,1,0:T(8,128)(2,1)S(1)}, bf16[1,3,256,128]{3,2,1,0:T(8,128)(2,1)S(1)}, u32[]{:S(2)}, u32[]{:S(2)}) collective-permute-start(bf16[1,3,256,128]{3,2,1,0:T(8,128)(2,1)S(1)} %bitcast.2), channel_id=1, source_target_pairs={{0,4},{2,6},{4,0},{6,2},{8,12},{10,14},{12,8},{14,10},{1,5},{3,7},... | collective-permute-start | bytes 589832 | tf_op jit(solution)/shard_map/ppermute | solution.py:297
  25.8 14.4 %collective-permute-start.4 = (bf16[1,3,256,128]{3,2,1,0:T(8,128)(2,1)S(1)}, bf16[1,3,256,128]{3,2,1,0:T(8,128)(2,1)S(1)}, u32[]{:S(2)}, u32[]{:S(2)}) collective-permute-start(bf16[1,3,256,128]{3,2,1,0:T(8,128)(2,1)S(1)} %bitcast.3), channel_id=1, source_target_pairs={{0,8},{2,10},{4,12},{6,14},{8,0},{10,2},{12,4},{14,6},{1,9},{3,11}... | collective-permute-start | bytes 589832 | tf_op jit(solution)/shard_map/ppermute | solution.py:297
  27.9 17.7 %collective-permute-start.3 = (bf16[1,3,256,128]{3,2,1,0:T(8,128)(2,1)S(1)}, bf16[1,3,256,128]{3,2,1,0:T(8,128)(2,1)S(1)}, u32[]{:S(2)}, u32[]{:S(2)}) collective-permute-start(bf16[1,3,256,128]{3,2,1,0:T(8,128)(2,1)S(1)} %bitcast.4), channel_id=1, source_target_pairs={{0,12},{2,14},{4,8},{6,10},{8,4},{10,6},{12,0},{14,2},{1,13},{3,15... | collective-permute-start | bytes 589832 | tf_op jit(solution)/shard_map/ppermute | solution.py:297
  48.9 7.8 %collective-permute-start.6 = (f32[12,384]{1,0:T(8,128)S(1)}, f32[12,384]{1,0:T(8,128)S(1)}, u32[]{:S(2)}, u32[]{:S(2)}) collective-permute-start(f32[12,384]{1,0:T(8,128)S(1)} %get-tuple-element.15), channel_id=1, source_target_pairs={{0,1},{1,0},{2,3},{3,2},{4,5},{5,4},{6,7},{7,6},{8,9},{9,8},{10,11... | collective-permute-start | bytes 55304 | tf_op jit(solution)/shard_map/ppermute | solution.py:318
  50.1 7.4 %collective-permute-start.7 = (f32[12,384]{1,0:T(8,128)S(1)}, f32[12,384]{1,0:T(8,128)S(1)}, u32[]{:S(2)}, u32[]{:S(2)}) collective-permute-start(f32[12,384]{1,0:T(8,128)S(1)} %get-tuple-element.16), channel_id=1, source_target_pairs={{0,2},{2,0},{4,6},{6,4},{8,10},{10,8},{12,14},{14,12},{1,3},{3,1},... | collective-permute-start | bytes 55304 | tf_op jit(solution)/shard_map/ppermute | solution.py:319
  56.4 3.8 %collective-permute-start.8 = (f32[12,384]{1,0:T(8,128)S(1)}, f32[12,384]{1,0:T(8,128)S(1)}, u32[]{:S(2)}, u32[]{:S(2)}) collective-permute-start(f32[12,384]{1,0:T(8,128)S(1)} %get-tuple-element.16), channel_id=1, source_target_pairs={{0,3},{1,2},{2,1},{3,0},{4,7},{5,6},{6,5},{7,4},{8,11},{9,10},{10,... | collective-permute-start | bytes 55304 | tf_op jit(solution)/shard_map/ppermute | solution.py:319
where the time goes:
time: 61 us; the launch traced here: 60.8 us
  starting transfers between devices  20.7 us (34%)
  Pallas kernels  19.8 us (32%)
  waiting for transfers between devices  19.5 us (32%)
  other arithmetic  0.62 us (1%)
    pallas_call x4, Pallas kernels, share_scores(): pl.pallas_call(lambda *refs: score_kernel(slots, caps, share, last, *refs...  16.4 us
    ppermute x1, waiting for transfers between devices, per_device(): pair_bank = lax.ppermute(video_bank, 'vid', swap_pair)  12.7 us
    ppermute x1, starting transfers between devices, per_device(): lax.ppermute(far, 'vid', swap_pair)  6.22 us
    all_to_all x1, starting transfers between devices, per_device(): shares = lax.all_to_all(pieces, 'vid', 0, 0, tiled=True)  5.73 us
    ppermute x3, waiting for transfers between devices, per_device(): arrived.append(lax.ppermute(wanted, 'vid', steps))  3.32 us
    ppermute x3, starting transfers between devices, per_device(): arrived.append(lax.ppermute(wanted, 'vid', steps))  2.71 us
    ppermute x1, waiting for transfers between devices, per_device(): lax.ppermute(far, ('vid', 'tok'), swap_both)  2.57 us
    pallas_call x1, Pallas kernels, per_device(): pl.pallas_call(lambda *refs: prepare_kernel('tok', *refs), in_specs=[pl.B...  1.9 us
  transfers between devices with their start and end apart: 10, of which 5 were waited for; matrix products, arithmetic and copies ran while one was open for 0% of the time, Pallas kernels for 24%

commit v1 on v0

--- a/solution.py
+++ b/solution.py
@@ -168,15 +168,19 @@
     )(meta, meta, query, bank, *past)
 
 
-def merge_kernel(caps, blocks, inner, quarters, vid_axis, tok_axis, order_ref, own_ref, tok_ref,
-                 pair_ref, both_ref, counts_ref, bank_ref, meta_ref, sems):
+def merge_kernel(own_ref, tok_ref, pair_ref, both_ref, bank_ref, sems):
     videos, half = own_ref.shape[:2]
-    rounds = order_ref.shape[0]
     moves = []
     for k, src in enumerate((own_ref, tok_ref, pair_ref, both_ref)):
         dst = bank_ref.at[pl.ds(k // 2 * videos, videos), pl.ds(k % 2 * half, half), :]
         moves.append(pltpu.make_async_copy(src, dst, sems.at[k]))
         moves[-1].start()
+    for move in moves:
+        move.wait()
+
+
+def tables_kernel(caps, blocks, inner, quarters, vid_axis, tok_axis, counts_ref, meta_ref):
+    rounds = counts_ref.shape[0]
     vid = lax.axis_index(vid_axis)
     quarter = vid % PAIR * (quarters // PAIR) + lax.axis_index(tok_axis)
     place = vid // PAIR % inner
@@ -204,8 +208,6 @@
     meta_ref[1:2, :] = counts[:1].astype(jnp.int32)
     meta_ref[2:3, :] = jnp.where(used, turn * LANES + cap, -1)
     meta_ref[3:4, :] = totals[:1].astype(jnp.int32)
-    for move in moves:
-        move.wait()
 
 
 def prepare_kernel(tok_axis, block_ref, counts_ref, out_ref, piece_ref, count_ref, in_sems, out_sems):
@@ -257,6 +259,7 @@
 
     tok_bank = lax.ppermute(video_bank, "tok", swap_tok)
     pair_bank = lax.ppermute(video_bank, "vid", swap_pair)
+    both_bank = lax.ppermute(pair_bank, "tok", swap_tok)
 
     pieces = pl.pallas_call(
         lambda *refs: prepare_kernel("tok", *refs),
@@ -272,6 +275,15 @@
         name="prepare",
     )(captions.reshape(n_vid, n_tok, rows, width), caption_lengths)
     shares = lax.all_to_all(pieces, "vid", 0, 0, tiled=True)
+    bank = pl.pallas_call(
+        merge_kernel,
+        in_specs=[pl.BlockSpec(memory_space=pl.ANY)] * 4,
+        out_specs=vmem,
+        out_shape=jax.ShapeDtypeStruct((2 * videos, 2 * half, width), video_bank.dtype),
+        scratch_shapes=[pltpu.SemaphoreType.DMA((4,))],
+        compiler_params=small,
+        name="merge",
+    )(video_bank, tok_bank, pair_bank, both_bank)
     wanted, counts = pl.pallas_call(
         pick_kernel,
         in_specs=[pl.BlockSpec(memory_space=pltpu.SMEM), vmem],
@@ -296,21 +308,14 @@
         steps = [(i, i ^ (k * PAIR)) for i in range(n_vid)]
         arrived.append(lax.ppermute(wanted, "vid", steps))
 
-    both_bank = lax.ppermute(pair_bank, "tok", swap_tok)
-    bank, meta = pl.pallas_call(
-        lambda *refs: merge_kernel(caps, blocks, inner, PAIR * n_tok, "vid", "tok", *refs),
-        in_specs=[pl.BlockSpec(memory_space=pltpu.SMEM)]
-        + [pl.BlockSpec(memory_space=pl.ANY)] * 4
-        + [vmem],
-        out_specs=[vmem] * 2,
-        out_shape=[
-            jax.ShapeDtypeStruct((2 * videos, 2 * half, width), video_bank.dtype),
-            jax.ShapeDtypeStruct((8, LANES), jnp.int32),
-        ],
-        scratch_shapes=[pltpu.SemaphoreType.DMA((4,))],
+    meta = pl.pallas_call(
+        lambda *refs: tables_kernel(caps, blocks, inner, PAIR * n_tok, "vid", "tok", *refs),
+        in_specs=[vmem],
+        out_specs=vmem,
+        out_shape=jax.ShapeDtypeStruct((8, LANES), jnp.int32),
         compiler_params=small,
-        name="merge",
-    )(owner_order, video_bank, tok_bank, pair_bank, both_bank, counts)
+        name="tables",
+    )(counts)
     total = ()
     for k, query in enumerate(arrived):
         total = share_scores(slots, caps, k, k == inner - 1, meta, query, bank, *total)

time: 61 us -> 62.9 us (1.031)
  the two profiles are of different devices: /device:TPU:11 before, /device:TPU:30 now
where the time goes in v1:
time: 62.9 us; the launch traced here: 62.7 us
  waiting for transfers between devices  26.5 us (42%)
  starting transfers between devices  19.6 us (31%)
  Pallas kernels  15.9 us (25%)
    ppermute x1, waiting for transfers between devices, per_device(): pair_bank = lax.ppermute(video_bank, 'vid', swap_pair)  14.2 us
    pallas_call x4, Pallas kernels, share_scores(): pl.pallas_call(lambda *refs: score_kernel(slots, caps, share, last, *refs...  12.9 us
    ppermute x1, starting transfers between devices, per_device(): lax.ppermute(far, ('vid', 'tok'), swap_both)  8.4 us
    ppermute x3, waiting for transfers between devices, per_device(): arrived.append(lax.ppermute(wanted, 'vid', steps))  6.84 us
    all_to_all x1, starting transfers between devices, per_device(): shares = lax.all_to_all(pieces, 'vid', 0, 0, tiled=True)  6.01 us
    ppermute x3, starting transfers between devices, per_device(): arrived.append(lax.ppermute(wanted, 'vid', steps))  4.45 us
    ppermute x1, waiting for transfers between devices, per_device(): lax.ppermute(far, 'vid', swap_pair)  2.31 us
    pallas_call x1, Pallas kernels, per_device(): pl.pallas_call(lambda *refs: prepare_kernel('tok', *refs), in_specs=[pl.B...  1.89 us
  transfers between devices with their start and end apart: 10, of which 6 were waited for; matrix products, arithmetic and copies ran while one was open for 0% of the time, Pallas kernels for 16%

profile of v1, /device:TPU:30, one launch (start us, length us, event | category | flops | bytes accessed | tf_op | source)
XLA Modules:
  0.0 62.7 jit_solution(9937788983577599437)
XLA Ops:
  0.0 0.0 copy-start
  0.0 1.9 %prepare.1 = bf16[8,264,128]{2,1,0:T(8,128)(2,1)} custom-call(bf16[8,2,256,128]{3,2,1,0:T(8,128)(2,1)} %bitcast.6, s32[1,128]{1,0:T(1,128)} %refs_1_.1), custom_call_target="tpu_custom_call" | custom-call | tf_op jit(solution)/shard_map/prepare/pallas_call | solution.py:264
  1.9 6.0 %all-to-all-start = ((bf16[8,264,128]{2,1,0:T(8,128)(2,1)}), bf16[8,264,128]{2,1,0:T(8,128)(2,1)S(1)}, u32[]{:S(2)}, u32[]{:S(2)}) async-start(bf16[8,264,128]{2,1,0:T(8,128)(2,1)} %prepare.1), calls=%async_computation | async-start | bytes 1081344 | tf_op jit(solution)/shard_map/all_to_all | solution.py:277
  7.9 0.0 copy-done
  7.9 0.0 copy-start.1
  7.9 0.6 collective-permute-start.2
  8.5 0.0 collective-permute-start.1
  8.5 14.2 %collective-permute-done.2.pair_ref = bf16[12,128,128]{2,1,0:T(8,128)(2,1)S(1)} collective-permute-done((bf16[12,128,128]{2,1,0:T(8,128)(2,1)S(1)}, bf16[12,128,128]{2,1,0:T(8,128)(2,1)S(1)}, u32[]{:S(2)}, u32[]{:S(2)}) %collective-permute-start.2) | collective-permute-done | bytes 393248 | tf_op jit(solution)/shard_map/ppermute | solution.py:261
  22.7 0.0 collective-permute-start.3
  22.8 0.0 collective-permute-done.1.tok_ref
  22.8 1.7 %collective-permute-done.3.both_ref = bf16[12,128,128]{2,1,0:T(8,128)(2,1)S(1)} collective-permute-done((bf16[12,128,128]{2,1,0:T(8,128)(2,1)S(1)}, bf16[12,128,128]{2,1,0:T(8,128)(2,1)S(1)}, u32[]{:S(2)}, u32[]{:S(2)}) %collective-permute-start.3) | collective-permute-done | bytes 393248 | tf_op jit(solution)/shard_map/ppermute | solution.py:262
  24.5 0.1 merge.1.refs_3_
  24.6 0.0 all-to-all-done.shares_ref
  24.6 0.0 copy-done.1
  24.6 0.6 pick.1
  25.2 0.9 %collective-permute-start.5 = (bf16[1,3,256,128]{3,2,1,0:T(8,128)(2,1)S(1)}, bf16[1,3,256,128]{3,2,1,0:T(8,128)(2,1)S(1)}, u32[]{:S(2)}, u32[]{:S(2)}) collective-permute-start(bf16[1,3,256,128]{3,2,1,0:T(8,128)(2,1)S(1)} %bitcast.2), channel_id=1, source_target_pairs={{0,4},{2,6},{4,0},{6,2},{8,12},{10,14},{12,8},{14,10},{1,5},{3,7},... | collective-permute-start | bytes 589832 | tf_op jit(solution)/shard_map/ppermute | solution.py:309
  26.1 0.7 %collective-permute-start.4 = (bf16[1,3,256,128]{3,2,1,0:T(8,128)(2,1)S(1)}, bf16[1,3,256,128]{3,2,1,0:T(8,128)(2,1)S(1)}, u32[]{:S(2)}, u32[]{:S(2)}) collective-permute-start(bf16[1,3,256,128]{3,2,1,0:T(8,128)(2,1)S(1)} %bitcast.3), channel_id=1, source_target_pairs={{0,8},{2,10},{4,12},{6,14},{8,0},{10,2},{12,4},{14,6},{1,9},{3,11}... | collective-permute-start | bytes 589832 | tf_op jit(solution)/shard_map/ppermute | solution.py:309
  26.8 2.8 %collective-permute-start = (bf16[1,3,256,128]{3,2,1,0:T(8,128)(2,1)S(1)}, bf16[1,3,256,128]{3,2,1,0:T(8,128)(2,1)S(1)}, u32[]{:S(2)}, u32[]{:S(2)}) collective-permute-start(bf16[1,3,256,128]{3,2,1,0:T(8,128)(2,1)S(1)} %bitcast.4), channel_id=1, source_target_pairs={{0,12},{2,14},{4,8},{6,10},{8,4},{10,6},{12,0},{14,2},{1,13},{3,15... | collective-permute-start | bytes 589832 | tf_op jit(solution)/shard_map/ppermute | solution.py:309
  29.7 0.3 tables.1.refs_0_.refs_1_
  30.0 3.2 %soft_scores.4.refs_4_ = f32[24,128]{1,0:T(8,128)S(1)} custom-call(s32[8,128]{1,0:T(8,128)S(1)} %tables.1.refs_0_.refs_1_, s32[8,128]{1,0:T(8,128)S(1)} %tables.1.refs_0_.refs_1_, bf16[1,3,256,128]{3,2,1,0:T(8,128)(2,1)S(1)} %bitcast.5, bf16[24,256,128]{2,1,0:T(8,128)(2,1)S(1)} %merge.1.refs_3_), custom_call_target="tpu_custom_call" | custom-call | flops 2415919104 | bytes 1572864 | tf_op jit(solution)/shard_map/soft_scores/pallas_call | solution.py:150
  33.2 2.1 %collective-permute-done.5.refs_2_ = bf16[1,3,256,128]{3,2,1,0:T(8,128)(2,1)S(1)} collective-permute-done((bf16[1,3,256,128]{3,2,1,0:T(8,128)(2,1)S(1)}, bf16[1,3,256,128]{3,2,1,0:T(8,128)(2,1)S(1)}, u32[]{:S(2)}, u32[]{:S(2)}) %collective-permute-start.5) | collective-permute-done | bytes 196640 | tf_op jit(solution)/shard_map/ppermute | solution.py:309
  35.3 3.2 %soft_scores.5.refs_4_ = f32[24,128]{1,0:T(8,128)S(1)} custom-call(s32[8,128]{1,0:T(8,128)S(1)} %tables.1.refs_0_.refs_1_, s32[8,128]{1,0:T(8,128)S(1)} %tables.1.refs_0_.refs_1_, bf16[1,3,256,128]{3,2,1,0:T(8,128)(2,1)S(1)} %collective-permute-done.5.refs_2_, bf16[24,256,128]{2,1,0:T(8,128)(2,1)S(1)} %merge.1.refs_3_, f32[24,128]{1,0:T(8,128)S(1)} %soft_scores.4.refs_4_), custom_call_target="tpu_custom_call" | custom-call | flops 2415919104 | bytes 1572864 | tf_op jit(solution)/shard_map/soft_scores/pallas_call | solution.py:150
  38.5 4.7 %collective-permute-done.4.refs_2_ = bf16[1,3,256,128]{3,2,1,0:T(8,128)(2,1)S(1)} collective-permute-done((bf16[1,3,256,128]{3,2,1,0:T(8,128)(2,1)S(1)}, bf16[1,3,256,128]{3,2,1,0:T(8,128)(2,1)S(1)}, u32[]{:S(2)}, u32[]{:S(2)}) %collective-permute-start.4) | collective-permute-done | bytes 196640 | tf_op jit(solution)/shard_map/ppermute | solution.py:309
  43.2 3.2 %soft_scores.6.refs_4_ = f32[24,128]{1,0:T(8,128)S(1)} custom-call(s32[8,128]{1,0:T(8,128)S(1)} %tables.1.refs_0_.refs_1_, s32[8,128]{1,0:T(8,128)S(1)} %tables.1.refs_0_.refs_1_, bf16[1,3,256,128]{3,2,1,0:T(8,128)(2,1)S(1)} %collective-permute-done.4.refs_2_, bf16[24,256,128]{2,1,0:T(8,128)(2,1)S(1)} %merge.1.refs_3_, f32[24,128]{1,0:T(8,128)S(1)} %soft_scores.5.refs_4_), custom_call_target="tpu_custom_call" | custom-call | flops 2415919104 | bytes 1572864 | tf_op jit(solution)/shard_map/soft_scores/pallas_call | solution.py:150
  46.4 0.0 collective-permute-done.refs_2_
  46.4 3.4 %soft_scores.7 = (f32[12,384]{1,0:T(8,128)S(1)}, f32[12,384]{1,0:T(8,128)S(1)}) custom-call(s32[8,128]{1,0:T(8,128)S(1)} %tables.1.refs_0_.refs_1_, s32[8,128]{1,0:T(8,128)S(1)} %tables.1.refs_0_.refs_1_, bf16[1,3,256,128]{3,2,1,0:T(8,128)(2,1)S(1)} %collective-permute-done.refs_2_, bf16[24,256,128]{2,1,0:T(8,128)(2,1)S(1)} %merge.1.refs_3_, ...), custom_call_target="tpu_custom_call" | custom-call | flops 2415919104 | bytes 1572864 | tf_op jit(solution)/shard_map/soft_scores/pallas_call | solution.py:150
  49.8 0.1 collective-permute-start.6
  49.9 8.4 %collective-permute-start.8 = (f32[12,384]{1,0:T(8,128)S(1)}, f32[12,384]{1,0:T(8,128)S(1)}, u32[]{:S(2)}, u32[]{:S(2)}) collective-permute-start(f32[12,384]{1,0:T(8,128)S(1)} %get-tuple-element.12), channel_id=1, source_target_pairs={{0,3},{1,2},{2,1},{3,0},{4,7},{5,6},{6,5},{7,4},{8,11},{9,10},{10,... | collective-permute-start | bytes 55304 | tf_op jit(solution)/shard_map/ppermute | solution.py:324
  58.3 0.0 collective-permute-start.7
  58.3 0.0 collective-permute-done.6
  58.3 1.5 %collective-permute-done.8 = f32[12,384]{1,0:T(8,128)S(1)} collective-permute-done((f32[12,384]{1,0:T(8,128)S(1)}, f32[12,384]{1,0:T(8,128)S(1)}, u32[]{:S(2)}, u32[]{:S(2)}) %collective-permute-start.8) | collective-permute-done | bytes 18464 | tf_op jit(solution)/shard_map/ppermute | solution.py:324
  59.8 2.3 %collective-permute-done.7 = f32[12,384]{1,0:T(8,128)S(1)} collective-permute-done((f32[12,384]{1,0:T(8,128)S(1)}, f32[12,384]{1,0:T(8,128)S(1)}, u32[]{:S(2)}, u32[]{:S(2)}) %collective-permute-start.7) | collective-permute-done | bytes 18464 | tf_op jit(solution)/shard_map/ppermute | solution.py:324
  62.1 0.6 add_add_fusion
Async XLA Ops:
  0.0 7.9 %copy-start = (bf16[12,128,128]{2,1,0:T(8,128)(2,1)S(1)}, bf16[12,128,128]{2,1,0:T(8,128)(2,1)}, u32[]{:S(2)}) copy-start(bf16[12,128,128]{2,1,0:T(8,128)(2,1)} %own_ref.1) | copy-start | bytes 1179652
  1.9 22.7 %all-to-all-start = ((bf16[8,264,128]{2,1,0:T(8,128)(2,1)}), bf16[8,264,128]{2,1,0:T(8,128)(2,1)S(1)}, u32[]{:S(2)}, u32[]{:S(2)}) async-start(bf16[8,264,128]{2,1,0:T(8,128)(2,1)} %prepare.1), calls=%async_computation | async-start | bytes 1081344 | tf_op jit(solution)/shard_map/all_to_all | solution.py:277
  7.9 16.7 %copy-start.1 = (s32[3]{0:T(128)S(1)}, s32[3]{0:T(128)}, u32[]{:S(2)}) copy-start(s32[3]{0:T(128)} %order_ref.1) | copy-start | bytes 40
  7.9 14.8 %collective-permute-start.2 = (bf16[12,128,128]{2,1,0:T(8,128)(2,1)S(1)}, bf16[12,128,128]{2,1,0:T(8,128)(2,1)S(1)}, u32[]{:S(2)}, u32[]{:S(2)}) collective-permute-start(bf16[12,128,128]{2,1,0:T(8,128)(2,1)S(1)} %copy-done), channel_id=1, source_target_pairs={{0,2},{2,0},{4,6},{6,4},{8,10},{10,8},{12,14},{14,12},{1,3},{3,1},... | collective-permute-start | bytes 1179656 | tf_op jit(solution)/shard_map/ppermute | solution.py:261
  8.5 14.2 %collective-permute-start.1 = (bf16[12,128,128]{2,1,0:T(8,128)(2,1)S(1)}, bf16[12,128,128]{2,1,0:T(8,128)(2,1)S(1)}, u32[]{:S(2)}, u32[]{:S(2)}) collective-permute-start(bf16[12,128,128]{2,1,0:T(8,128)(2,1)S(1)} %copy-done), channel_id=1, source_target_pairs={{0,1},{1,0},{2,3},{3,2},{4,5},{5,4},{6,7},{7,6},{8,9},{9,8},{10,11... | collective-permute-start | bytes 1179656 | tf_op jit(solution)/shard_map/ppermute | solution.py:260
  22.7 1.7 %collective-permute-start.3 = (bf16[12,128,128]{2,1,0:T(8,128)(2,1)S(1)}, bf16[12,128,128]{2,1,0:T(8,128)(2,1)S(1)}, u32[]{:S(2)}, u32[]{:S(2)}) collective-permute-start(bf16[12,128,128]{2,1,0:T(8,128)(2,1)S(1)} %collective-permute-done.2.pair_ref), channel_id=1, source_target_pairs={{0,1},{1,0},{2,3},{3,2},{4,5},{5,4},{6,7},{7,6},{8,9},{9,8},{10,11... | collective-permute-start | bytes 1179656 | tf_op jit(solution)/shard_map/ppermute | solution.py:262
  25.2 10.1 %collective-permute-start.5 = (bf16[1,3,256,128]{3,2,1,0:T(8,128)(2,1)S(1)}, bf16[1,3,256,128]{3,2,1,0:T(8,128)(2,1)S(1)}, u32[]{:S(2)}, u32[]{:S(2)}) collective-permute-start(bf16[1,3,256,128]{3,2,1,0:T(8,128)(2,1)S(1)} %bitcast.2), channel_id=1, source_target_pairs={{0,4},{2,6},{4,0},{6,2},{8,12},{10,14},{12,8},{14,10},{1,5},{3,7},... | collective-permute-start | bytes 589832 | tf_op jit(solution)/shard_map/ppermute | solution.py:309
  26.1 17.1 %collective-permute-start.4 = (bf16[1,3,256,128]{3,2,1,0:T(8,128)(2,1)S(1)}, bf16[1,3,256,128]{3,2,1,0:T(8,128)(2,1)S(1)}, u32[]{:S(2)}, u32[]{:S(2)}) collective-permute-start(bf16[1,3,256,128]{3,2,1,0:T(8,128)(2,1)S(1)} %bitcast.3), channel_id=1, source_target_pairs={{0,8},{2,10},{4,12},{6,14},{8,0},{10,2},{12,4},{14,6},{1,9},{3,11}... | collective-permute-start | bytes 589832 | tf_op jit(solution)/shard_map/ppermute | solution.py:309
  26.8 19.6 %collective-permute-start = (bf16[1,3,256,128]{3,2,1,0:T(8,128)(2,1)S(1)}, bf16[1,3,256,128]{3,2,1,0:T(8,128)(2,1)S(1)}, u32[]{:S(2)}, u32[]{:S(2)}) collective-permute-start(bf16[1,3,256,128]{3,2,1,0:T(8,128)(2,1)S(1)} %bitcast.4), channel_id=1, source_target_pairs={{0,12},{2,14},{4,8},{6,10},{8,4},{10,6},{12,0},{14,2},{1,13},{3,15... | collective-permute-start | bytes 589832 | tf_op jit(solution)/shard_map/ppermute | solution.py:309
  49.8 8.5 %collective-permute-start.6 = (f32[12,384]{1,0:T(8,128)S(1)}, f32[12,384]{1,0:T(8,128)S(1)}, u32[]{:S(2)}, u32[]{:S(2)}) collective-permute-start(f32[12,384]{1,0:T(8,128)S(1)} %get-tuple-element.11), channel_id=1, source_target_pairs={{0,1},{1,0},{2,3},{3,2},{4,5},{5,4},{6,7},{7,6},{8,9},{9,8},{10,11... | collective-permute-start | bytes 55304 | tf_op jit(solution)/shard_map/ppermute | solution.py:323
  49.9 9.9 %collective-permute-start.8 = (f32[12,384]{1,0:T(8,128)S(1)}, f32[12,384]{1,0:T(8,128)S(1)}, u32[]{:S(2)}, u32[]{:S(2)}) collective-permute-start(f32[12,384]{1,0:T(8,128)S(1)} %get-tuple-element.12), channel_id=1, source_target_pairs={{0,3},{1,2},{2,1},{3,0},{4,7},{5,6},{6,5},{7,4},{8,11},{9,10},{10,... | collective-permute-start | bytes 55304 | tf_op jit(solution)/shard_map/ppermute | solution.py:324
  58.3 3.8 %collective-permute-start.7 = (f32[12,384]{1,0:T(8,128)S(1)}, f32[12,384]{1,0:T(8,128)S(1)}, u32[]{:S(2)}, u32[]{:S(2)}) collective-permute-start(f32[12,384]{1,0:T(8,128)S(1)} %get-tuple-element.12), channel_id=1, source_target_pairs={{0,2},{2,0},{4,6},{6,4},{8,10},{10,8},{12,14},{14,12},{1,3},{3,1},... | collective-permute-start | bytes 55304 | tf_op jit(solution)/shard_map/ppermute | solution.py:324

commit v2 on v1

--- a/solution.py
+++ b/solution.py
@@ -213,22 +213,30 @@
 def prepare_kernel(tok_axis, block_ref, counts_ref, out_ref, piece_ref, count_ref, in_sems, out_sems):
     n, rows = block_ref.shape[0], block_ref.shape[2]
     tok = lax.axis_index(tok_axis)
-    lengths = pltpu.make_async_copy(counts_ref, count_ref, in_sems.at[n])
+    lengths = pltpu.make_async_copy(counts_ref, count_ref, in_sems.at[2 * n])
     lengths.start()
+    part = rows // 2
+    parts = [(i, h) for i in range(n) for h in range(2)]
     moves = []
-    for k in range(n):
+    for k, (i, h) in enumerate(parts):
+        spot = pl.ds(h * part, part)
         moves.append(
-            pltpu.make_async_copy(block_ref.at[k, tok], piece_ref.at[k, pl.ds(0, rows)], in_sems.at[k])
+            pltpu.make_async_copy(block_ref.at[i, tok, spot], piece_ref.at[i, spot], in_sems.at[k])
         )
         moves[-1].start()
+    for k, (i, h) in enumerate(parts):
+        moves[k].wait()
+        spot = pl.ds(h * part, part)
+        moves[k] = pltpu.make_async_copy(piece_ref.at[i, spot], out_ref.at[i, spot], out_sems.at[k])
+        moves[k].start()
     lengths.wait()
     counts = jnp.broadcast_to(count_ref[...], (COUNT_ROWS, LANES)).astype(F32).astype(BF16)
-    for k in range(n):
-        piece_ref[k, rows:, :] = counts
-    for k in range(n):
-        moves[k].wait()
-        moves[k] = pltpu.make_async_copy(piece_ref.at[k], out_ref.at[k], out_sems.at[k])
-        moves[k].start()
+    piece_ref[0, rows:, :] = counts
+    for i in range(n):
+        tail = piece_ref.at[0, pl.ds(rows, COUNT_ROWS)]
+        spot = pl.ds(rows, COUNT_ROWS)
+        moves.append(pltpu.make_async_copy(tail, out_ref.at[i, spot], out_sems.at[2 * n + i]))
+        moves[-1].start()
     for move in moves:
         move.wait()
 
@@ -269,8 +277,8 @@
         scratch_shapes=[
             pltpu.VMEM((n_vid, rows + COUNT_ROWS, width), captions.dtype),
             pltpu.VMEM(caption_lengths.shape, caption_lengths.dtype),
-            pltpu.SemaphoreType.DMA((n_vid + 1,)),
-            pltpu.SemaphoreType.DMA((n_vid,)),
+            pltpu.SemaphoreType.DMA((2 * n_vid + 1,)),
+            pltpu.SemaphoreType.DMA((3 * n_vid,)),
         ],
         name="prepare",
     )(captions.reshape(n_vid, n_tok, rows, width), caption_lengths)

time: 62.9 us -> 63.1 us (level)
  no operation moved by 1% of the time
where the time goes in v2:
time: 63.1 us; the launch traced here: 62.9 us
  waiting for transfers between devices  26.5 us (42%)
  starting transfers between devices  19.6 us (31%)
  Pallas kernels  16 us (25%)
    ppermute x1, waiting for transfers between devices, per_device(): pair_bank = lax.ppermute(video_bank, 'vid', swap_pair)  14.2 us
    pallas_call x4, Pallas kernels, share_scores(): pl.pallas_call(lambda *refs: score_kernel(slots, caps, share, last, *refs...  13 us
    ppermute x1, starting transfers between devices, per_device(): lax.ppermute(far, ('vid', 'tok'), swap_both)  8.41 us
    ppermute x3, waiting for transfers between devices, per_device(): arrived.append(lax.ppermute(wanted, 'vid', steps))  6.83 us
    all_to_all x1, starting transfers between devices, per_device(): shares = lax.all_to_all(pieces, 'vid', 0, 0, tiled=True)  6.01 us
    ppermute x3, starting transfers between devices, per_device(): arrived.append(lax.ppermute(wanted, 'vid', steps))  4.45 us
    ppermute x1, waiting for transfers between devices, per_device(): lax.ppermute(far, 'vid', swap_pair)  2.31 us
    pallas_call x1, Pallas kernels, per_device(): pl.pallas_call(lambda *refs: prepare_kernel('tok', *refs), in_specs=[pl.B...  2.06 us
  transfers between devices with their start and end apart: 10, of which 6 were waited for; matrix products, arithmetic and copies ran while one was open for 0% of the time, Pallas kernels for 16%

profile of v2, /device:TPU:30, one launch (start us, length us, event | category | flops | bytes accessed | tf_op | source)
XLA Modules:
  0.0 62.9 jit_solution(8948209708921297285)
XLA Ops:
  0.0 0.0 copy-start
  0.0 2.1 %prepare.1 = bf16[8,264,128]{2,1,0:T(8,128)(2,1)} custom-call(bf16[8,2,256,128]{3,2,1,0:T(8,128)(2,1)} %bitcast.6, s32[1,128]{1,0:T(1,128)} %refs_1_.1), custom_call_target="tpu_custom_call" | custom-call | tf_op jit(solution)/shard_map/prepare/pallas_call | solution.py:272
  2.1 6.0 %all-to-all-start = ((bf16[8,264,128]{2,1,0:T(8,128)(2,1)}), bf16[8,264,128]{2,1,0:T(8,128)(2,1)S(1)}, u32[]{:S(2)}, u32[]{:S(2)}) async-start(bf16[8,264,128]{2,1,0:T(8,128)(2,1)} %prepare.1), calls=%async_computation | async-start | bytes 1081344 | tf_op jit(solution)/shard_map/all_to_all | solution.py:285
  8.1 0.0 copy-done
  8.1 0.0 copy-start.1
  8.1 0.6 collective-permute-start.2
  8.7 0.0 collective-permute-start.1
  8.7 14.2 %collective-permute-done.2.pair_ref = bf16[12,128,128]{2,1,0:T(8,128)(2,1)S(1)} collective-permute-done((bf16[12,128,128]{2,1,0:T(8,128)(2,1)S(1)}, bf16[12,128,128]{2,1,0:T(8,128)(2,1)S(1)}, u32[]{:S(2)}, u32[]{:S(2)}) %collective-permute-start.2) | collective-permute-done | bytes 393248 | tf_op jit(solution)/shard_map/ppermute | solution.py:269
  22.9 0.0 collective-permute-start.3
  22.9 0.0 collective-permute-done.1.tok_ref
  22.9 1.7 %collective-permute-done.3.both_ref = bf16[12,128,128]{2,1,0:T(8,128)(2,1)S(1)} collective-permute-done((bf16[12,128,128]{2,1,0:T(8,128)(2,1)S(1)}, bf16[12,128,128]{2,1,0:T(8,128)(2,1)S(1)}, u32[]{:S(2)}, u32[]{:S(2)}) %collective-permute-start.3) | collective-permute-done | bytes 393248 | tf_op jit(solution)/shard_map/ppermute | solution.py:270
  24.6 0.1 merge.1.refs_3_
  24.8 0.0 all-to-all-done.shares_ref
  24.8 0.0 copy-done.1
  24.8 0.6 pick.1
  25.4 0.9 %collective-permute-start.5 = (bf16[1,3,256,128]{3,2,1,0:T(8,128)(2,1)S(1)}, bf16[1,3,256,128]{3,2,1,0:T(8,128)(2,1)S(1)}, u32[]{:S(2)}, u32[]{:S(2)}) collective-permute-start(bf16[1,3,256,128]{3,2,1,0:T(8,128)(2,1)S(1)} %bitcast.2), channel_id=1, source_target_pairs={{0,4},{2,6},{4,0},{6,2},{8,12},{10,14},{12,8},{14,10},{1,5},{3,7},... | collective-permute-start | bytes 589832 | tf_op jit(solution)/shard_map/ppermute | solution.py:317
  26.3 0.7 %collective-permute-start.4 = (bf16[1,3,256,128]{3,2,1,0:T(8,128)(2,1)S(1)}, bf16[1,3,256,128]{3,2,1,0:T(8,128)(2,1)S(1)}, u32[]{:S(2)}, u32[]{:S(2)}) collective-permute-start(bf16[1,3,256,128]{3,2,1,0:T(8,128)(2,1)S(1)} %bitcast.3), channel_id=1, source_target_pairs={{0,8},{2,10},{4,12},{6,14},{8,0},{10,2},{12,4},{14,6},{1,9},{3,11}... | collective-permute-start | bytes 589832 | tf_op jit(solution)/shard_map/ppermute | solution.py:317
  27.0 2.8 %collective-permute-start = (bf16[1,3,256,128]{3,2,1,0:T(8,128)(2,1)S(1)}, bf16[1,3,256,128]{3,2,1,0:T(8,128)(2,1)S(1)}, u32[]{:S(2)}, u32[]{:S(2)}) collective-permute-start(bf16[1,3,256,128]{3,2,1,0:T(8,128)(2,1)S(1)} %bitcast.4), channel_id=1, source_target_pairs={{0,12},{2,14},{4,8},{6,10},{8,4},{10,6},{12,0},{14,2},{1,13},{3,15... | collective-permute-start | bytes 589832 | tf_op jit(solution)/shard_map/ppermute | solution.py:317
  29.8 0.3 tables.1.refs_0_.refs_1_
  30.1 3.2 %soft_scores.4.refs_4_ = f32[24,128]{1,0:T(8,128)S(1)} custom-call(s32[8,128]{1,0:T(8,128)S(1)} %tables.1.refs_0_.refs_1_, s32[8,128]{1,0:T(8,128)S(1)} %tables.1.refs_0_.refs_1_, bf16[1,3,256,128]{3,2,1,0:T(8,128)(2,1)S(1)} %bitcast.5, bf16[24,256,128]{2,1,0:T(8,128)(2,1)S(1)} %merge.1.refs_3_), custom_call_target="tpu_custom_call" | custom-call | flops 2415919104 | bytes 1572864 | tf_op jit(solution)/shard_map/soft_scores/pallas_call | solution.py:150
  33.4 2.1 %collective-permute-done.5.refs_2_ = bf16[1,3,256,128]{3,2,1,0:T(8,128)(2,1)S(1)} collective-permute-done((bf16[1,3,256,128]{3,2,1,0:T(8,128)(2,1)S(1)}, bf16[1,3,256,128]{3,2,1,0:T(8,128)(2,1)S(1)}, u32[]{:S(2)}, u32[]{:S(2)}) %collective-permute-start.5) | collective-permute-done | bytes 196640 | tf_op jit(solution)/shard_map/ppermute | solution.py:317
  35.5 3.2 %soft_scores.5.refs_4_ = f32[24,128]{1,0:T(8,128)S(1)} custom-call(s32[8,128]{1,0:T(8,128)S(1)} %tables.1.refs_0_.refs_1_, s32[8,128]{1,0:T(8,128)S(1)} %tables.1.refs_0_.refs_1_, bf16[1,3,256,128]{3,2,1,0:T(8,128)(2,1)S(1)} %collective-permute-done.5.refs_2_, bf16[24,256,128]{2,1,0:T(8,128)(2,1)S(1)} %merge.1.refs_3_, f32[24,128]{1,0:T(8,128)S(1)} %soft_scores.4.refs_4_), custom_call_target="tpu_custom_call" | custom-call | flops 2415919104 | bytes 1572864 | tf_op jit(solution)/shard_map/soft_scores/pallas_call | solution.py:150
  38.7 4.7 %collective-permute-done.4.refs_2_ = bf16[1,3,256,128]{3,2,1,0:T(8,128)(2,1)S(1)} collective-permute-done((bf16[1,3,256,128]{3,2,1,0:T(8,128)(2,1)S(1)}, bf16[1,3,256,128]{3,2,1,0:T(8,128)(2,1)S(1)}, u32[]{:S(2)}, u32[]{:S(2)}) %collective-permute-start.4) | collective-permute-done | bytes 196640 | tf_op jit(solution)/shard_map/ppermute | solution.py:317
  43.4 3.2 %soft_scores.6.refs_4_ = f32[24,128]{1,0:T(8,128)S(1)} custom-call(s32[8,128]{1,0:T(8,128)S(1)} %tables.1.refs_0_.refs_1_, s32[8,128]{1,0:T(8,128)S(1)} %tables.1.refs_0_.refs_1_, bf16[1,3,256,128]{3,2,1,0:T(8,128)(2,1)S(1)} %collective-permute-done.4.refs_2_, bf16[24,256,128]{2,1,0:T(8,128)(2,1)S(1)} %merge.1.refs_3_, f32[24,128]{1,0:T(8,128)S(1)} %soft_scores.5.refs_4_), custom_call_target="tpu_custom_call" | custom-call | flops 2415919104 | bytes 1572864 | tf_op jit(solution)/shard_map/soft_scores/pallas_call | solution.py:150
  46.6 0.0 collective-permute-done.refs_2_
  46.6 3.4 %soft_scores.7 = (f32[12,384]{1,0:T(8,128)S(1)}, f32[12,384]{1,0:T(8,128)S(1)}) custom-call(s32[8,128]{1,0:T(8,128)S(1)} %tables.1.refs_0_.refs_1_, s32[8,128]{1,0:T(8,128)S(1)} %tables.1.refs_0_.refs_1_, bf16[1,3,256,128]{3,2,1,0:T(8,128)(2,1)S(1)} %collective-permute-done.refs_2_, bf16[24,256,128]{2,1,0:T(8,128)(2,1)S(1)} %merge.1.refs_3_, ...), custom_call_target="tpu_custom_call" | custom-call | flops 2415919104 | bytes 1572864 | tf_op jit(solution)/shard_map/soft_scores/pallas_call | solution.py:150
  50.0 0.1 collective-permute-start.6
  50.1 8.4 %collective-permute-start.8 = (f32[12,384]{1,0:T(8,128)S(1)}, f32[12,384]{1,0:T(8,128)S(1)}, u32[]{:S(2)}, u32[]{:S(2)}) collective-permute-start(f32[12,384]{1,0:T(8,128)S(1)} %get-tuple-element.12), channel_id=1, source_target_pairs={{0,3},{1,2},{2,1},{3,0},{4,7},{5,6},{6,5},{7,4},{8,11},{9,10},{10,... | collective-permute-start | bytes 55304 | tf_op jit(solution)/shard_map/ppermute | solution.py:332
  58.5 0.0 collective-permute-start.7
  58.5 0.0 collective-permute-done.6
  58.5 1.5 %collective-permute-done.8 = f32[12,384]{1,0:T(8,128)S(1)} collective-permute-done((f32[12,384]{1,0:T(8,128)S(1)}, f32[12,384]{1,0:T(8,128)S(1)}, u32[]{:S(2)}, u32[]{:S(2)}) %collective-permute-start.8) | collective-permute-done | bytes 18464 | tf_op jit(solution)/shard_map/ppermute | solution.py:332
  60.0 2.3 %collective-permute-done.7 = f32[12,384]{1,0:T(8,128)S(1)} collective-permute-done((f32[12,384]{1,0:T(8,128)S(1)}, f32[12,384]{1,0:T(8,128)S(1)}, u32[]{:S(2)}, u32[]{:S(2)}) %collective-permute-start.7) | collective-permute-done | bytes 18464 | tf_op jit(solution)/shard_map/ppermute | solution.py:332
  62.3 0.6 add_add_fusion
Async XLA Ops:
  0.0 8.1 %copy-start = (bf16[12,128,128]{2,1,0:T(8,128)(2,1)S(1)}, bf16[12,128,128]{2,1,0:T(8,128)(2,1)}, u32[]{:S(2)}) copy-start(bf16[12,128,128]{2,1,0:T(8,128)(2,1)} %own_ref.1) | copy-start | bytes 1179652
  2.1 22.7 %all-to-all-start = ((bf16[8,264,128]{2,1,0:T(8,128)(2,1)}), bf16[8,264,128]{2,1,0:T(8,128)(2,1)S(1)}, u32[]{:S(2)}, u32[]{:S(2)}) async-start(bf16[8,264,128]{2,1,0:T(8,128)(2,1)} %prepare.1), calls=%async_computation | async-start | bytes 1081344 | tf_op jit(solution)/shard_map/all_to_all | solution.py:285
  8.1 16.7 %copy-start.1 = (s32[3]{0:T(128)S(1)}, s32[3]{0:T(128)}, u32[]{:S(2)}) copy-start(s32[3]{0:T(128)} %order_ref.1) | copy-start | bytes 40
  8.1 14.8 %collective-permute-start.2 = (bf16[12,128,128]{2,1,0:T(8,128)(2,1)S(1)}, bf16[12,128,128]{2,1,0:T(8,128)(2,1)S(1)}, u32[]{:S(2)}, u32[]{:S(2)}) collective-permute-start(bf16[12,128,128]{2,1,0:T(8,128)(2,1)S(1)} %copy-done), channel_id=1, source_target_pairs={{0,2},{2,0},{4,6},{6,4},{8,10},{10,8},{12,14},{14,12},{1,3},{3,1},... | collective-permute-start | bytes 1179656 | tf_op jit(solution)/shard_map/ppermute | solution.py:269
  8.7 14.2 %collective-permute-start.1 = (bf16[12,128,128]{2,1,0:T(8,128)(2,1)S(1)}, bf16[12,128,128]{2,1,0:T(8,128)(2,1)S(1)}, u32[]{:S(2)}, u32[]{:S(2)}) collective-permute-start(bf16[12,128,128]{2,1,0:T(8,128)(2,1)S(1)} %copy-done), channel_id=1, source_target_pairs={{0,1},{1,0},{2,3},{3,2},{4,5},{5,4},{6,7},{7,6},{8,9},{9,8},{10,11... | collective-permute-start | bytes 1179656 | tf_op jit(solution)/shard_map/ppermute | solution.py:268
  22.9 1.7 %collective-permute-start.3 = (bf16[12,128,128]{2,1,0:T(8,128)(2,1)S(1)}, bf16[12,128,128]{2,1,0:T(8,128)(2,1)S(1)}, u32[]{:S(2)}, u32[]{:S(2)}) collective-permute-start(bf16[12,128,128]{2,1,0:T(8,128)(2,1)S(1)} %collective-permute-done.2.pair_ref), channel_id=1, source_target_pairs={{0,1},{1,0},{2,3},{3,2},{4,5},{5,4},{6,7},{7,6},{8,9},{9,8},{10,11... | collective-permute-start | bytes 1179656 | tf_op jit(solution)/shard_map/ppermute | solution.py:270
  25.4 10.1 %collective-permute-start.5 = (bf16[1,3,256,128]{3,2,1,0:T(8,128)(2,1)S(1)}, bf16[1,3,256,128]{3,2,1,0:T(8,128)(2,1)S(1)}, u32[]{:S(2)}, u32[]{:S(2)}) collective-permute-start(bf16[1,3,256,128]{3,2,1,0:T(8,128)(2,1)S(1)} %bitcast.2), channel_id=1, source_target_pairs={{0,4},{2,6},{4,0},{6,2},{8,12},{10,14},{12,8},{14,10},{1,5},{3,7},... | collective-permute-start | bytes 589832 | tf_op jit(solution)/shard_map/ppermute | solution.py:317
  26.3 17.1 %collective-permute-start.4 = (bf16[1,3,256,128]{3,2,1,0:T(8,128)(2,1)S(1)}, bf16[1,3,256,128]{3,2,1,0:T(8,128)(2,1)S(1)}, u32[]{:S(2)}, u32[]{:S(2)}) collective-permute-start(bf16[1,3,256,128]{3,2,1,0:T(8,128)(2,1)S(1)} %bitcast.3), channel_id=1, source_target_pairs={{0,8},{2,10},{4,12},{6,14},{8,0},{10,2},{12,4},{14,6},{1,9},{3,11}... | collective-permute-start | bytes 589832 | tf_op jit(solution)/shard_map/ppermute | solution.py:317
  27.0 19.6 %collective-permute-start = (bf16[1,3,256,128]{3,2,1,0:T(8,128)(2,1)S(1)}, bf16[1,3,256,128]{3,2,1,0:T(8,128)(2,1)S(1)}, u32[]{:S(2)}, u32[]{:S(2)}) collective-permute-start(bf16[1,3,256,128]{3,2,1,0:T(8,128)(2,1)S(1)} %bitcast.4), channel_id=1, source_target_pairs={{0,12},{2,14},{4,8},{6,10},{8,4},{10,6},{12,0},{14,2},{1,13},{3,15... | collective-permute-start | bytes 589832 | tf_op jit(solution)/shard_map/ppermute | solution.py:317
  50.0 8.5 %collective-permute-start.6 = (f32[12,384]{1,0:T(8,128)S(1)}, f32[12,384]{1,0:T(8,128)S(1)}, u32[]{:S(2)}, u32[]{:S(2)}) collective-permute-start(f32[12,384]{1,0:T(8,128)S(1)} %get-tuple-element.11), channel_id=1, source_target_pairs={{0,1},{1,0},{2,3},{3,2},{4,5},{5,4},{6,7},{7,6},{8,9},{9,8},{10,11... | collective-permute-start | bytes 55304 | tf_op jit(solution)/shard_map/ppermute | solution.py:331
  50.1 9.9 %collective-permute-start.8 = (f32[12,384]{1,0:T(8,128)S(1)}, f32[12,384]{1,0:T(8,128)S(1)}, u32[]{:S(2)}, u32[]{:S(2)}) collective-permute-start(f32[12,384]{1,0:T(8,128)S(1)} %get-tuple-element.12), channel_id=1, source_target_pairs={{0,3},{1,2},{2,1},{3,0},{4,7},{5,6},{6,5},{7,4},{8,11},{9,10},{10,... | collective-permute-start | bytes 55304 | tf_op jit(solution)/shard_map/ppermute | solution.py:332
  58.5 3.8 %collective-permute-start.7 = (f32[12,384]{1,0:T(8,128)S(1)}, f32[12,384]{1,0:T(8,128)S(1)}, u32[]{:S(2)}, u32[]{:S(2)}) collective-permute-start(f32[12,384]{1,0:T(8,128)S(1)} %get-tuple-element.12), channel_id=1, source_target_pairs={{0,2},{2,0},{4,6},{6,4},{8,10},{10,8},{12,14},{14,12},{1,3},{3,1},... | collective-permute-start | bytes 55304 | tf_op jit(solution)/shard_map/ppermute | solution.py:332

commit v3 on v0

--- a/solution.py
+++ b/solution.py
@@ -169,7 +169,7 @@
 
 
 def merge_kernel(caps, blocks, inner, quarters, vid_axis, tok_axis, order_ref, own_ref, tok_ref,
-                 pair_ref, both_ref, counts_ref, bank_ref, meta_ref, sems):
+                 pair_ref, both_ref, shares_ref, bank_ref, meta_ref, sems):
     videos, half = own_ref.shape[:2]
     rounds = order_ref.shape[0]
     moves = []
@@ -194,7 +194,8 @@
     counts = jnp.zeros((COUNT_ROWS, LANES), F32)
     for r in range(rounds):
         pick = jnp.where((down == cap) & (turn == r) & used, F32(1), F32(0)).astype(BF16)
-        counts = counts + dot(counts_ref[r], pick, ((1,), (0,)))
+        lengths = shares_ref[order_ref[r], shares_ref.shape[1] - COUNT_ROWS :, :]
+        counts = counts + dot(lengths, pick, ((1,), (0,)))
     before = jnp.where((down < across) & (down // per == share), F32(1), F32(0)).astype(BF16)
     within = jnp.where(down // per == across, F32(1), F32(0)).astype(BF16)
     starts = dot(counts.astype(BF16), before, ((1,), (0,)))
@@ -231,14 +232,6 @@
         move.wait()
 
 
-def pick_kernel(order_ref, shares_ref, wanted_ref, counts_ref):
-    rows = shares_ref.shape[1] - COUNT_ROWS
-    for r in range(order_ref.shape[0]):
-        owner = order_ref[r]
-        wanted_ref[r * rows : (r + 1) * rows, :] = shares_ref[owner, :rows, :]
-        counts_ref[r] = shares_ref[owner, rows:, :]
-
-
 def per_device(captions, caption_lengths, video_bank, owner_order):
     n_vid, n_tok = lax.axis_size("vid"), lax.axis_size("tok")
     capb, slots, width = captions.shape[1:]
@@ -272,17 +265,9 @@
         name="prepare",
     )(captions.reshape(n_vid, n_tok, rows, width), caption_lengths)
     shares = lax.all_to_all(pieces, "vid", 0, 0, tiled=True)
-    wanted, counts = pl.pallas_call(
-        pick_kernel,
-        in_specs=[pl.BlockSpec(memory_space=pltpu.SMEM), vmem],
-        out_specs=[vmem] * 2,
-        out_shape=[
-            jax.ShapeDtypeStruct((rounds * rows, width), captions.dtype),
-            jax.ShapeDtypeStruct((rounds, COUNT_ROWS, width), captions.dtype),
-        ],
-        compiler_params=small,
-        name="pick",
-    )(owner_order, shares)
+    wanted = jnp.concatenate(
+        [lax.dynamic_index_in_dim(shares, owner_order[r], 0, keepdims=False)[:rows] for r in range(rounds)]
+    )
     inner = min(STEPS, line)
     blocks = line // inner
     if blocks > 1:
@@ -310,7 +295,7 @@
         scratch_shapes=[pltpu.SemaphoreType.DMA((4,))],
         compiler_params=small,
         name="merge",
-    )(owner_order, video_bank, tok_bank, pair_bank, both_bank, counts)
+    )(owner_order, video_bank, tok_bank, pair_bank, both_bank, shares)
     total = ()
     for k, query in enumerate(arrived):
         total = share_scores(slots, caps, k, k == inner - 1, meta, query, bank, *total)

time: 61 us -> 73 us (1.20)
  the two profiles are of different devices: /device:TPU:11 before, /device:TPU:10 now
where the time goes in v3:
time: 73 us; the launch traced here: 72.7 us
  waiting for transfers between devices  27.8 us (38%)
  starting transfers between devices  22 us (30%)
  Pallas kernels  15.8 us (22%)
  between operations  5.82 us (8%)
    ppermute x1, waiting for transfers between devices, per_device(): pair_bank = lax.ppermute(video_bank, 'vid', swap_pair)  14.5 us
    pallas_call x4, Pallas kernels, share_scores(): pl.pallas_call(lambda *refs: score_kernel(slots, caps, share, last, *refs...  12.9 us
    ppermute x1, starting transfers between devices, per_device(): lax.ppermute(far, ('vid', 'tok'), swap_both)  10.1 us
    ppermute x3, waiting for transfers between devices, per_device(): arrived.append(lax.ppermute(wanted, 'vid', steps))  9.57 us
    all_to_all x1, starting transfers between devices, per_device(): shares = lax.all_to_all(pieces, 'vid', 0, 0, tiled=True)  6.29 us
    ppermute x3, starting transfers between devices, per_device(): arrived.append(lax.ppermute(wanted, 'vid', steps))  3.89 us
    ppermute x1, waiting for transfers between devices, per_device(): lax.ppermute(far, 'vid', swap_pair)  2.31 us
    pallas_call x1, Pallas kernels, per_device(): pl.pallas_call(lambda *refs: prepare_kernel('tok', *refs), in_specs=[pl.B...  1.89 us
  transfers between devices with their start and end apart: 10, of which 4 were waited for; matrix products, arithmetic and copies ran while one was open for 1% of the time, Pallas kernels for 15%

profile of v3, /device:TPU:10, one launch (start us, length us, event | category | flops | bytes accessed | tf_op | source)
XLA Modules:
  0.0 72.7 jit_solution(4494634986595058053)
XLA Ops:
  0.0 0.0 copy-start
  0.0 0.0 copy-start.1
  0.0 1.9 %prepare.1 = bf16[8,264,128]{2,1,0:T(8,128)(2,1)} custom-call(bf16[8,2,256,128]{3,2,1,0:T(8,128)(2,1)} %bitcast.15, s32[1,128]{1,0:T(1,128)} %refs_1_.2), custom_call_target="tpu_custom_call" | custom-call | tf_op jit(solution)/shard_map/prepare/pallas_call | solution.py:254
  1.9 6.3 %all-to-all-start = ((bf16[8,264,128]{2,1,0:T(8,128)(2,1)}), bf16[8,264,128]{2,1,0:T(8,128)(2,1)S(1)}, u32[]{:S(2)}, u32[]{:S(2)}) async-start(bf16[8,264,128]{2,1,0:T(8,128)(2,1)} %prepare.1), calls=%async_computation | async-start | bytes 1081344 | tf_op jit(solution)/shard_map/all_to_all | solution.py:267
  8.2 0.0 copy-done
  8.2 1.5 %collective-permute-start.1 = (bf16[12,128,128]{2,1,0:T(8,128)(2,1)S(1)}, bf16[12,128,128]{2,1,0:T(8,128)(2,1)S(1)}, u32[]{:S(2)}, u32[]{:S(2)}) collective-permute-start(bf16[12,128,128]{2,1,0:T(8,128)(2,1)S(1)} %copy-done), channel_id=1, source_target_pairs={{0,2},{2,0},{4,6},{6,4},{8,10},{10,8},{12,14},{14,12},{1,3},{3,1},... | collective-permute-start | bytes 1179656 | tf_op jit(solution)/shard_map/ppermute | solution.py:252
  9.7 0.0 collective-permute-start
  9.7 14.5 %collective-permute-done.1.refs_3_ = bf16[12,128,128]{2,1,0:T(8,128)(2,1)S(1)} collective-permute-done((bf16[12,128,128]{2,1,0:T(8,128)(2,1)S(1)}, bf16[12,128,128]{2,1,0:T(8,128)(2,1)S(1)}, u32[]{:S(2)}, u32[]{:S(2)}) %collective-permute-start.1) | collective-permute-done | bytes 393248 | tf_op jit(solution)/shard_map/ppermute | solution.py:252
  24.2 0.0 collective-permute-start.2
  24.2 0.0 copy-done.1
  24.2 0.7 fusion
  30.6 0.0 all-to-all-done.refs_5_
  30.6 1.5 %collective-permute-start.3 = (bf16[1,3,256,128]{3,2,1,0:T(8,128)(2,1)S(1)}, bf16[1,3,256,128]{3,2,1,0:T(8,128)(2,1)S(1)}, u32[]{:S(2)}, u32[]{:S(2)}) collective-permute-start(bf16[1,3,256,128]{3,2,1,0:T(8,128)(2,1)S(1)} %bitcast.11), channel_id=1, source_target_pairs={{0,12},{2,14},{4,8},{6,10},{8,4},{10,6},{12,0},{14,2},{1,13},{3,15... | collective-permute-start | bytes 589832 | tf_op jit(solution)/shard_map/ppermute | solution.py:282
  32.2 1.5 %collective-permute-start.4 = (bf16[1,3,256,128]{3,2,1,0:T(8,128)(2,1)S(1)}, bf16[1,3,256,128]{3,2,1,0:T(8,128)(2,1)S(1)}, u32[]{:S(2)}, u32[]{:S(2)}) collective-permute-start(bf16[1,3,256,128]{3,2,1,0:T(8,128)(2,1)S(1)} %bitcast.12), channel_id=1, source_target_pairs={{0,8},{2,10},{4,12},{6,14},{8,0},{10,2},{12,4},{14,6},{1,9},{3,11}... | collective-permute-start | bytes 589832 | tf_op jit(solution)/shard_map/ppermute | solution.py:282
  33.6 0.9 %collective-permute-start.5 = (bf16[1,3,256,128]{3,2,1,0:T(8,128)(2,1)S(1)}, bf16[1,3,256,128]{3,2,1,0:T(8,128)(2,1)S(1)}, u32[]{:S(2)}, u32[]{:S(2)}) collective-permute-start(bf16[1,3,256,128]{3,2,1,0:T(8,128)(2,1)S(1)} %bitcast.13), channel_id=1, source_target_pairs={{0,4},{2,6},{4,0},{6,2},{8,12},{10,14},{12,8},{14,10},{1,5},{3,7},... | collective-permute-start | bytes 589832 | tf_op jit(solution)/shard_map/ppermute | solution.py:282
  34.5 0.0 collective-permute-done.refs_2_
  34.5 0.0 collective-permute-done.2.refs_4_
  34.5 1.0 %merge.1 = (bf16[24,256,128]{2,1,0:T(8,128)(2,1)S(1)}, s32[8,128]{1,0:T(8,128)S(1)}) custom-call(s32[3]{0:T(128)S(1)} %copy-done.1, bf16[12,128,128]{2,1,0:T(8,128)(2,1)S(1)} %copy-done, bf16[12,128,128]{2,1,0:T(8,128)(2,1)S(1)} %collective-permute-done.refs_2_, bf16[12,128,128]{2,1,0:T(8,128)(2,1)S(1)} %collective-permute-done.1.refs_3_, ...), custom_call_target="tpu_custom_call" | custom-call | tf_op jit(solution)/shard_map/merge/pallas_call | solution.py:285
  35.6 3.2 %soft_scores.4.refs_4_ = f32[24,128]{1,0:T(8,128)S(1)} custom-call(s32[8,128]{1,0:T(8,128)S(1)} %get-tuple-element.9.refs_0_.refs_1_, s32[8,128]{1,0:T(8,128)S(1)} %get-tuple-element.9.refs_0_.refs_1_, bf16[1,3,256,128]{3,2,1,0:T(8,128)(2,1)S(1)} %bitcast.14, bf16[24,256,128]{2,1,0:T(8,128)(2,1)S(1)} %get-tuple-element.10.refs_3_), custom_call_target="tpu_custom_call" | custom-call | flops 2415919104 | bytes 1572864 | tf_op jit(solution)/shard_map/soft_scores/pallas_call | solution.py:150
  38.8 9.6 %collective-permute-done.5.refs_2_ = bf16[1,3,256,128]{3,2,1,0:T(8,128)(2,1)S(1)} collective-permute-done((bf16[1,3,256,128]{3,2,1,0:T(8,128)(2,1)S(1)}, bf16[1,3,256,128]{3,2,1,0:T(8,128)(2,1)S(1)}, u32[]{:S(2)}, u32[]{:S(2)}) %collective-permute-start.5) | collective-permute-done | bytes 196640 | tf_op jit(solution)/shard_map/ppermute | solution.py:282
  48.3 3.2 %soft_scores.5.refs_4_ = f32[24,128]{1,0:T(8,128)S(1)} custom-call(s32[8,128]{1,0:T(8,128)S(1)} %get-tuple-element.9.refs_0_.refs_1_, s32[8,128]{1,0:T(8,128)S(1)} %get-tuple-element.9.refs_0_.refs_1_, bf16[1,3,256,128]{3,2,1,0:T(8,128)(2,1)S(1)} %collective-permute-done.5.refs_2_, bf16[24,256,128]{2,1,0:T(8,128)(2,1)S(1)} %get-tuple-element.10.refs_3_, ...), custom_call_target="tpu_custom_call" | custom-call | flops 2415919104 | bytes 1572864 | tf_op jit(solution)/shard_map/soft_scores/pallas_call | solution.py:150
  51.5 0.0 collective-permute-done.4.refs_2_
  51.5 3.2 %soft_scores.6.refs_4_ = f32[24,128]{1,0:T(8,128)S(1)} custom-call(s32[8,128]{1,0:T(8,128)S(1)} %get-tuple-element.9.refs_0_.refs_1_, s32[8,128]{1,0:T(8,128)S(1)} %get-tuple-element.9.refs_0_.refs_1_, bf16[1,3,256,128]{3,2,1,0:T(8,128)(2,1)S(1)} %collective-permute-done.4.refs_2_, bf16[24,256,128]{2,1,0:T(8,128)(2,1)S(1)} %get-tuple-element.10.refs_3_, ...), custom_call_target="tpu_custom_call" | custom-call | flops 2415919104 | bytes 1572864 | tf_op jit(solution)/shard_map/soft_scores/pallas_call | solution.py:150
  54.7 0.0 collective-permute-done.3.refs_2_
  54.8 3.4 %soft_scores.7 = (f32[12,384]{1,0:T(8,128)S(1)}, f32[12,384]{1,0:T(8,128)S(1)}) custom-call(s32[8,128]{1,0:T(8,128)S(1)} %get-tuple-element.9.refs_0_.refs_1_, s32[8,128]{1,0:T(8,128)S(1)} %get-tuple-element.9.refs_0_.refs_1_, bf16[1,3,256,128]{3,2,1,0:T(8,128)(2,1)S(1)} %collective-permute-done.3.refs_2_, ...), custom_call_target="tpu_custom_call" | custom-call | flops 2415919104 | bytes 1572864 | tf_op jit(solution)/shard_map/soft_scores/pallas_call | solution.py:150
  58.1 10.1 %collective-permute-start.8 = (f32[12,384]{1,0:T(8,128)S(1)}, f32[12,384]{1,0:T(8,128)S(1)}, u32[]{:S(2)}, u32[]{:S(2)}) collective-permute-start(f32[12,384]{1,0:T(8,128)S(1)} %get-tuple-element.12), channel_id=1, source_target_pairs={{0,3},{1,2},{2,1},{3,0},{4,7},{5,6},{6,5},{7,4},{8,11},{9,10},{10,... | collective-permute-start | bytes 55304 | tf_op jit(solution)/shard_map/ppermute | solution.py:304
  68.2 0.0 collective-permute-start.7
  68.2 0.2 collective-permute-start.6
  68.4 1.3 %collective-permute-done.8 = f32[12,384]{1,0:T(8,128)S(1)} collective-permute-done((f32[12,384]{1,0:T(8,128)S(1)}, f32[12,384]{1,0:T(8,128)S(1)}, u32[]{:S(2)}, u32[]{:S(2)}) %collective-permute-start.8) | collective-permute-done | bytes 18464 | tf_op jit(solution)/shard_map/ppermute | solution.py:304
  69.8 2.3 %collective-permute-done.7 = f32[12,384]{1,0:T(8,128)S(1)} collective-permute-done((f32[12,384]{1,0:T(8,128)S(1)}, f32[12,384]{1,0:T(8,128)S(1)}, u32[]{:S(2)}, u32[]{:S(2)}) %collective-permute-start.7) | collective-permute-done | bytes 18464 | tf_op jit(solution)/shard_map/ppermute | solution.py:304
  72.1 0.0 collective-permute-done.6
  72.1 0.6 add_add_fusion
  (2 shorter events, 0.0 us)
Async XLA Ops:
  0.0 8.2 %copy-start = (bf16[12,128,128]{2,1,0:T(8,128)(2,1)S(1)}, bf16[12,128,128]{2,1,0:T(8,128)(2,1)}, u32[]{:S(2)}) copy-start(bf16[12,128,128]{2,1,0:T(8,128)(2,1)} %refs_1_.3) | copy-start | bytes 1179652
  0.0 24.2 %copy-start.1 = (s32[3]{0:T(128)S(1)}, s32[3]{0:T(128)}, u32[]{:S(2)}) copy-start(s32[3]{0:T(128)} %refs_0_.1) | copy-start | bytes 40
  1.9 28.7 %all-to-all-start = ((bf16[8,264,128]{2,1,0:T(8,128)(2,1)}), bf16[8,264,128]{2,1,0:T(8,128)(2,1)S(1)}, u32[]{:S(2)}, u32[]{:S(2)}) async-start(bf16[8,264,128]{2,1,0:T(8,128)(2,1)} %prepare.1), calls=%async_computation | async-start | bytes 1081344 | tf_op jit(solution)/shard_map/all_to_all | solution.py:267
  8.2 16.0 %collective-permute-start.1 = (bf16[12,128,128]{2,1,0:T(8,128)(2,1)S(1)}, bf16[12,128,128]{2,1,0:T(8,128)(2,1)S(1)}, u32[]{:S(2)}, u32[]{:S(2)}) collective-permute-start(bf16[12,128,128]{2,1,0:T(8,128)(2,1)S(1)} %copy-done), channel_id=1, source_target_pairs={{0,2},{2,0},{4,6},{6,4},{8,10},{10,8},{12,14},{14,12},{1,3},{3,1},... | collective-permute-start | bytes 1179656 | tf_op jit(solution)/shard_map/ppermute | solution.py:252
  9.7 24.9 %collective-permute-start = (bf16[12,128,128]{2,1,0:T(8,128)(2,1)S(1)}, bf16[12,128,128]{2,1,0:T(8,128)(2,1)S(1)}, u32[]{:S(2)}, u32[]{:S(2)}) collective-permute-start(bf16[12,128,128]{2,1,0:T(8,128)(2,1)S(1)} %copy-done), channel_id=1, source_target_pairs={{0,1},{1,0},{2,3},{3,2},{4,5},{5,4},{6,7},{7,6},{8,9},{9,8},{10,11... | collective-permute-start | bytes 1179656 | tf_op jit(solution)/shard_map/ppermute | solution.py:251
  24.2 10.3 %collective-permute-start.2 = (bf16[12,128,128]{2,1,0:T(8,128)(2,1)S(1)}, bf16[12,128,128]{2,1,0:T(8,128)(2,1)S(1)}, u32[]{:S(2)}, u32[]{:S(2)}) collective-permute-start(bf16[12,128,128]{2,1,0:T(8,128)(2,1)S(1)} %collective-permute-done.1.refs_3_), channel_id=1, source_target_pairs={{0,1},{1,0},{2,3},{3,2},{4,5},{5,4},{6,7},{7,6},{8,9},{9,8},{10,11... | collective-permute-start | bytes 1179656 | tf_op jit(solution)/shard_map/ppermute | solution.py:284
  30.6 24.1 %collective-permute-start.3 = (bf16[1,3,256,128]{3,2,1,0:T(8,128)(2,1)S(1)}, bf16[1,3,256,128]{3,2,1,0:T(8,128)(2,1)S(1)}, u32[]{:S(2)}, u32[]{:S(2)}) collective-permute-start(bf16[1,3,256,128]{3,2,1,0:T(8,128)(2,1)S(1)} %bitcast.11), channel_id=1, source_target_pairs={{0,12},{2,14},{4,8},{6,10},{8,4},{10,6},{12,0},{14,2},{1,13},{3,15... | collective-permute-start | bytes 589832 | tf_op jit(solution)/shard_map/ppermute | solution.py:282
  32.2 19.4 %collective-permute-start.4 = (bf16[1,3,256,128]{3,2,1,0:T(8,128)(2,1)S(1)}, bf16[1,3,256,128]{3,2,1,0:T(8,128)(2,1)S(1)}, u32[]{:S(2)}, u32[]{:S(2)}) collective-permute-start(bf16[1,3,256,128]{3,2,1,0:T(8,128)(2,1)S(1)} %bitcast.12), channel_id=1, source_target_pairs={{0,8},{2,10},{4,12},{6,14},{8,0},{10,2},{12,4},{14,6},{1,9},{3,11}... | collective-permute-start | bytes 589832 | tf_op jit(solution)/shard_map/ppermute | solution.py:282
  33.6 14.7 %collective-permute-start.5 = (bf16[1,3,256,128]{3,2,1,0:T(8,128)(2,1)S(1)}, bf16[1,3,256,128]{3,2,1,0:T(8,128)(2,1)S(1)}, u32[]{:S(2)}, u32[]{:S(2)}) collective-permute-start(bf16[1,3,256,128]{3,2,1,0:T(8,128)(2,1)S(1)} %bitcast.13), channel_id=1, source_target_pairs={{0,4},{2,6},{4,0},{6,2},{8,12},{10,14},{12,8},{14,10},{1,5},{3,7},... | collective-permute-start | bytes 589832 | tf_op jit(solution)/shard_map/ppermute | solution.py:282
  58.1 11.6 %collective-permute-start.8 = (f32[12,384]{1,0:T(8,128)S(1)}, f32[12,384]{1,0:T(8,128)S(1)}, u32[]{:S(2)}, u32[]{:S(2)}) collective-permute-start(f32[12,384]{1,0:T(8,128)S(1)} %get-tuple-element.12), channel_id=1, source_target_pairs={{0,3},{1,2},{2,1},{3,0},{4,7},{5,6},{6,5},{7,4},{8,11},{9,10},{10,... | collective-permute-start | bytes 55304 | tf_op jit(solution)/shard_map/ppermute | solution.py:304
  68.2 3.8 %collective-permute-start.7 = (f32[12,384]{1,0:T(8,128)S(1)}, f32[12,384]{1,0:T(8,128)S(1)}, u32[]{:S(2)}, u32[]{:S(2)}) collective-permute-start(f32[12,384]{1,0:T(8,128)S(1)} %get-tuple-element.12), channel_id=1, source_target_pairs={{0,2},{2,0},{4,6},{6,4},{8,10},{10,8},{12,14},{14,12},{1,3},{3,1},... | collective-permute-start | bytes 55304 | tf_op jit(solution)/shard_map/ppermute | solution.py:304
  68.2 3.8 %collective-permute-start.6 = (f32[12,384]{1,0:T(8,128)S(1)}, f32[12,384]{1,0:T(8,128)S(1)}, u32[]{:S(2)}, u32[]{:S(2)}) collective-permute-start(f32[12,384]{1,0:T(8,128)S(1)} %get-tuple-element.11), channel_id=1, source_target_pairs={{0,1},{1,0},{2,3},{3,2},{4,5},{5,4},{6,7},{7,6},{8,9},{9,8},{10,11... | collective-permute-start | bytes 55304 | tf_op jit(solution)/shard_map/ppermute | solution.py:303

commit v4 on v3

--- a/solution.py
+++ b/solution.py
@@ -39,7 +39,7 @@
 def score_kernel(slots, caps, share, last, meta_ref, lanes_ref, q_ref, bank_ref, *refs):
     past, refs = (refs[:1], refs[1:]) if share else ((), refs)
     outs, refs = refs[: 1 + last], refs[1 + last :]
-    out_ref, (rows_ref, soft_ref, bad_ref, a_ref, b_ref) = refs[0] if last else outs[0], refs[last:]
+    out_ref, (rows_ref, soft_ref, bad_ref, a_ref, b_ref, w_ref) = refs[0] if last else outs[0], refs[last:]
     blocks, rounds = q_ref.shape[:2]
     videos, tokens = bank_ref.shape[0] // 2, bank_ref.shape[1]
     total_rows = meta_ref[3, share]
@@ -99,10 +99,15 @@
         out_ref[...] += got[:n] + got[n : 2 * n] + got[2 * n :]
 
     def tile(shifted, i, carry):
-        w = weights(i)
+        w = w_ref[...]
         collect(i - 1, shifted)
         for j, (base, size) in enumerate(jobs):
-            after = (jobs[j + 1], w) if j + 1 < len(jobs) else (jobs[0], weights(i + 1))
+            if j + 1 < len(jobs):
+                after = (jobs[j + 1], w)
+            else:
+                nxt = weights(i + 1)
+                w_ref[...] = nxt
+                after = (jobs[0], nxt)
             products(bufs[(j + 1) % 2], *after)
             for v in range(size):
                 for col in range(0, TILE, LANES):
@@ -117,7 +122,9 @@
 
     def run(shifted):
         out_ref[...] = past[0][...] if past else jnp.zeros_like(out_ref)
-        products(bufs[0], jobs[0], weights(0))
+        w0 = weights(0)
+        w_ref[...] = w0
+        products(bufs[0], jobs[0], w0)
         lax.fori_loop(0, tiles, functools.partial(tile, shifted), 0)
         collect(tiles - 1, shifted)
 
@@ -159,6 +166,7 @@
             pltpu.VMEM((2 * videos, TILE), F32),
             pltpu.VMEM((FIRST_JOB * tokens, TILE), F32),
             pltpu.VMEM(((2 * videos - FIRST_JOB) * tokens, TILE), F32),
+            pltpu.VMEM((TILE, 2 * width), BF16),
         ],
         compiler_params=pltpu.CompilerParams(vmem_limit_bytes=VMEM_BYTES),
         cost_estimate=pl.CostEstimate(

time: 73 us -> 72.8 us (level)
  transfers between devices with their start and end apart: 10 -> 10, of which waited for: 4 -> 4; matrix products, arithmetic and copies ran while one was open for 1% -> 1% of each run, Pallas kernels for 15% -> 14%
where the time goes in v4:
time: 72.8 us; the launch traced here: 72.5 us
  waiting for transfers between devices  27.8 us (38%)
  starting transfers between devices  21.9 us (30%)
  Pallas kernels  15.7 us (22%)
  between operations  5.82 us (8%)
    ppermute x1, waiting for transfers between devices, per_device(): pair_bank = lax.ppermute(video_bank, 'vid', swap_pair)  14.5 us
    pallas_call x4, Pallas kernels, share_scores(): pl.pallas_call(lambda *refs: score_kernel(slots, caps, share, last, *refs...  12.8 us
    ppermute x1, starting transfers between devices, per_device(): lax.ppermute(far, ('vid', 'tok'), swap_both)  10.1 us
    ppermute x3, waiting for transfers between devices, per_device(): arrived.append(lax.ppermute(wanted, 'vid', steps))  9.61 us
    all_to_all x1, starting transfers between devices, per_device(): shares = lax.all_to_all(pieces, 'vid', 0, 0, tiled=True)  6.29 us
    ppermute x3, starting transfers between devices, per_device(): arrived.append(lax.ppermute(wanted, 'vid', steps))  3.89 us
    ppermute x1, waiting for transfers between devices, per_device(): lax.ppermute(far, 'vid', swap_pair)  2.31 us
    pallas_call x1, Pallas kernels, per_device(): pl.pallas_call(lambda *refs: prepare_kernel('tok', *refs), in_specs=[pl.B...  1.89 us
  transfers between devices with their start and end apart: 10, of which 4 were waited for; matrix products, arithmetic and copies ran while one was open for 1% of the time, Pallas kernels for 14%

profile of v4, /device:TPU:10, one launch (start us, length us, event | category | flops | bytes accessed | tf_op | source)
XLA Modules:
  0.0 72.5 jit_solution(16437369285406503301)
XLA Ops:
  0.0 0.0 copy-start
  0.0 0.0 copy-start.1
  0.0 1.9 %prepare.1 = bf16[8,264,128]{2,1,0:T(8,128)(2,1)} custom-call(bf16[8,2,256,128]{3,2,1,0:T(8,128)(2,1)} %bitcast.15, s32[1,128]{1,0:T(1,128)} %refs_1_.2), custom_call_target="tpu_custom_call" | custom-call | tf_op jit(solution)/shard_map/prepare/pallas_call | solution.py:262
  1.9 6.3 %all-to-all-start = ((bf16[8,264,128]{2,1,0:T(8,128)(2,1)}), bf16[8,264,128]{2,1,0:T(8,128)(2,1)S(1)}, u32[]{:S(2)}, u32[]{:S(2)}) async-start(bf16[8,264,128]{2,1,0:T(8,128)(2,1)} %prepare.1), calls=%async_computation | async-start | bytes 1081344 | tf_op jit(solution)/shard_map/all_to_all | solution.py:275
  8.2 0.0 copy-done
  8.2 1.5 %collective-permute-start.1 = (bf16[12,128,128]{2,1,0:T(8,128)(2,1)S(1)}, bf16[12,128,128]{2,1,0:T(8,128)(2,1)S(1)}, u32[]{:S(2)}, u32[]{:S(2)}) collective-permute-start(bf16[12,128,128]{2,1,0:T(8,128)(2,1)S(1)} %copy-done), channel_id=1, source_target_pairs={{0,2},{2,0},{4,6},{6,4},{8,10},{10,8},{12,14},{14,12},{1,3},{3,1},... | collective-permute-start | bytes 1179656 | tf_op jit(solution)/shard_map/ppermute | solution.py:260
  9.7 0.0 collective-permute-start
  9.7 14.5 %collective-permute-done.1.refs_3_ = bf16[12,128,128]{2,1,0:T(8,128)(2,1)S(1)} collective-permute-done((bf16[12,128,128]{2,1,0:T(8,128)(2,1)S(1)}, bf16[12,128,128]{2,1,0:T(8,128)(2,1)S(1)}, u32[]{:S(2)}, u32[]{:S(2)}) %collective-permute-start.1) | collective-permute-done | bytes 393248 | tf_op jit(solution)/shard_map/ppermute | solution.py:260
  24.2 0.0 collective-permute-start.2
  24.2 0.0 copy-done.1
  24.2 0.7 fusion
  30.6 0.0 all-to-all-done.refs_5_
  30.6 1.5 %collective-permute-start.3 = (bf16[1,3,256,128]{3,2,1,0:T(8,128)(2,1)S(1)}, bf16[1,3,256,128]{3,2,1,0:T(8,128)(2,1)S(1)}, u32[]{:S(2)}, u32[]{:S(2)}) collective-permute-start(bf16[1,3,256,128]{3,2,1,0:T(8,128)(2,1)S(1)} %bitcast.11), channel_id=1, source_target_pairs={{0,12},{2,14},{4,8},{6,10},{8,4},{10,6},{12,0},{14,2},{1,13},{3,15... | collective-permute-start | bytes 589832 | tf_op jit(solution)/shard_map/ppermute | solution.py:290
  32.2 1.5 %collective-permute-start.4 = (bf16[1,3,256,128]{3,2,1,0:T(8,128)(2,1)S(1)}, bf16[1,3,256,128]{3,2,1,0:T(8,128)(2,1)S(1)}, u32[]{:S(2)}, u32[]{:S(2)}) collective-permute-start(bf16[1,3,256,128]{3,2,1,0:T(8,128)(2,1)S(1)} %bitcast.12), channel_id=1, source_target_pairs={{0,8},{2,10},{4,12},{6,14},{8,0},{10,2},{12,4},{14,6},{1,9},{3,11}... | collective-permute-start | bytes 589832 | tf_op jit(solution)/shard_map/ppermute | solution.py:290
  33.6 0.9 %collective-permute-start.5 = (bf16[1,3,256,128]{3,2,1,0:T(8,128)(2,1)S(1)}, bf16[1,3,256,128]{3,2,1,0:T(8,128)(2,1)S(1)}, u32[]{:S(2)}, u32[]{:S(2)}) collective-permute-start(bf16[1,3,256,128]{3,2,1,0:T(8,128)(2,1)S(1)} %bitcast.13), channel_id=1, source_target_pairs={{0,4},{2,6},{4,0},{6,2},{8,12},{10,14},{12,8},{14,10},{1,5},{3,7},... | collective-permute-start | bytes 589832 | tf_op jit(solution)/shard_map/ppermute | solution.py:290
  34.5 0.0 collective-permute-done.refs_2_
  34.5 0.0 collective-permute-done.2.refs_4_
  34.5 1.0 %merge.1 = (bf16[24,256,128]{2,1,0:T(8,128)(2,1)S(1)}, s32[8,128]{1,0:T(8,128)S(1)}) custom-call(s32[3]{0:T(128)S(1)} %copy-done.1, bf16[12,128,128]{2,1,0:T(8,128)(2,1)S(1)} %copy-done, bf16[12,128,128]{2,1,0:T(8,128)(2,1)S(1)} %collective-permute-done.refs_2_, bf16[12,128,128]{2,1,0:T(8,128)(2,1)S(1)} %collective-permute-done.1.refs_3_, ...), custom_call_target="tpu_custom_call" | custom-call | tf_op jit(solution)/shard_map/merge/pallas_call | solution.py:293
  35.6 3.2 %soft_scores.4.refs_4_ = f32[24,128]{1,0:T(8,128)S(1)} custom-call(s32[8,128]{1,0:T(8,128)S(1)} %get-tuple-element.9.refs_0_.refs_1_, s32[8,128]{1,0:T(8,128)S(1)} %get-tuple-element.9.refs_0_.refs_1_, bf16[1,3,256,128]{3,2,1,0:T(8,128)(2,1)S(1)} %bitcast.14, bf16[24,256,128]{2,1,0:T(8,128)(2,1)S(1)} %get-tuple-element.10.refs_3_), custom_call_target="tpu_custom_call" | custom-call | flops 2415919104 | bytes 1572864 | tf_op jit(solution)/shard_map/soft_scores/pallas_call | solution.py:157
  38.7 9.6 %collective-permute-done.5.refs_2_ = bf16[1,3,256,128]{3,2,1,0:T(8,128)(2,1)S(1)} collective-permute-done((bf16[1,3,256,128]{3,2,1,0:T(8,128)(2,1)S(1)}, bf16[1,3,256,128]{3,2,1,0:T(8,128)(2,1)S(1)}, u32[]{:S(2)}, u32[]{:S(2)}) %collective-permute-start.5) | collective-permute-done | bytes 196640 | tf_op jit(solution)/shard_map/ppermute | solution.py:290
  48.3 3.1 %soft_scores.5.refs_4_ = f32[24,128]{1,0:T(8,128)S(1)} custom-call(s32[8,128]{1,0:T(8,128)S(1)} %get-tuple-element.9.refs_0_.refs_1_, s32[8,128]{1,0:T(8,128)S(1)} %get-tuple-element.9.refs_0_.refs_1_, bf16[1,3,256,128]{3,2,1,0:T(8,128)(2,1)S(1)} %collective-permute-done.5.refs_2_, bf16[24,256,128]{2,1,0:T(8,128)(2,1)S(1)} %get-tuple-element.10.refs_3_, ...), custom_call_target="tpu_custom_call" | custom-call | flops 2415919104 | bytes 1572864 | tf_op jit(solution)/shard_map/soft_scores/pallas_call | solution.py:157
  51.5 0.0 collective-permute-done.4.refs_2_
  51.5 3.1 %soft_scores.6.refs_4_ = f32[24,128]{1,0:T(8,128)S(1)} custom-call(s32[8,128]{1,0:T(8,128)S(1)} %get-tuple-element.9.refs_0_.refs_1_, s32[8,128]{1,0:T(8,128)S(1)} %get-tuple-element.9.refs_0_.refs_1_, bf16[1,3,256,128]{3,2,1,0:T(8,128)(2,1)S(1)} %collective-permute-done.4.refs_2_, bf16[24,256,128]{2,1,0:T(8,128)(2,1)S(1)} %get-tuple-element.10.refs_3_, ...), custom_call_target="tpu_custom_call" | custom-call | flops 2415919104 | bytes 1572864 | tf_op jit(solution)/shard_map/soft_scores/pallas_call | solution.py:157
  54.7 0.0 collective-permute-done.3.refs_2_
  54.7 3.3 %soft_scores.7 = (f32[12,384]{1,0:T(8,128)S(1)}, f32[12,384]{1,0:T(8,128)S(1)}) custom-call(s32[8,128]{1,0:T(8,128)S(1)} %get-tuple-element.9.refs_0_.refs_1_, s32[8,128]{1,0:T(8,128)S(1)} %get-tuple-element.9.refs_0_.refs_1_, bf16[1,3,256,128]{3,2,1,0:T(8,128)(2,1)S(1)} %collective-permute-done.3.refs_2_, ...), custom_call_target="tpu_custom_call" | custom-call | flops 2415919104 | bytes 1572864 | tf_op jit(solution)/shard_map/soft_scores/pallas_call | solution.py:157
  58.0 10.1 %collective-permute-start.8 = (f32[12,384]{1,0:T(8,128)S(1)}, f32[12,384]{1,0:T(8,128)S(1)}, u32[]{:S(2)}, u32[]{:S(2)}) collective-permute-start(f32[12,384]{1,0:T(8,128)S(1)} %get-tuple-element.12), channel_id=1, source_target_pairs={{0,3},{1,2},{2,1},{3,0},{4,7},{5,6},{6,5},{7,4},{8,11},{9,10},{10,... | collective-permute-start | bytes 55304 | tf_op jit(solution)/shard_map/ppermute | solution.py:312
  68.1 0.0 collective-permute-start.7
  68.1 0.2 collective-permute-start.6
  68.3 1.3 %collective-permute-done.8 = f32[12,384]{1,0:T(8,128)S(1)} collective-permute-done((f32[12,384]{1,0:T(8,128)S(1)}, f32[12,384]{1,0:T(8,128)S(1)}, u32[]{:S(2)}, u32[]{:S(2)}) %collective-permute-start.8) | collective-permute-done | bytes 18464 | tf_op jit(solution)/shard_map/ppermute | solution.py:312
  69.6 2.3 %collective-permute-done.7 = f32[12,384]{1,0:T(8,128)S(1)} collective-permute-done((f32[12,384]{1,0:T(8,128)S(1)}, f32[12,384]{1,0:T(8,128)S(1)}, u32[]{:S(2)}, u32[]{:S(2)}) %collective-permute-start.7) | collective-permute-done | bytes 18464 | tf_op jit(solution)/shard_map/ppermute | solution.py:312
  71.9 0.0 collective-permute-done.6
  71.9 0.6 add_add_fusion
  (2 shorter events, 0.0 us)
Async XLA Ops:
  0.0 8.2 %copy-start = (bf16[12,128,128]{2,1,0:T(8,128)(2,1)S(1)}, bf16[12,128,128]{2,1,0:T(8,128)(2,1)}, u32[]{:S(2)}) copy-start(bf16[12,128,128]{2,1,0:T(8,128)(2,1)} %refs_1_.3) | copy-start | bytes 1179652
  0.0 24.2 %copy-start.1 = (s32[3]{0:T(128)S(1)}, s32[3]{0:T(128)}, u32[]{:S(2)}) copy-start(s32[3]{0:T(128)} %refs_0_.1) | copy-start | bytes 40
  1.9 28.7 %all-to-all-start = ((bf16[8,264,128]{2,1,0:T(8,128)(2,1)}), bf16[8,264,128]{2,1,0:T(8,128)(2,1)S(1)}, u32[]{:S(2)}, u32[]{:S(2)}) async-start(bf16[8,264,128]{2,1,0:T(8,128)(2,1)} %prepare.1), calls=%async_computation | async-start | bytes 1081344 | tf_op jit(solution)/shard_map/all_to_all | solution.py:275
  8.2 16.0 %collective-permute-start.1 = (bf16[12,128,128]{2,1,0:T(8,128)(2,1)S(1)}, bf16[12,128,128]{2,1,0:T(8,128)(2,1)S(1)}, u32[]{:S(2)}, u32[]{:S(2)}) collective-permute-start(bf16[12,128,128]{2,1,0:T(8,128)(2,1)S(1)} %copy-done), channel_id=1, source_target_pairs={{0,2},{2,0},{4,6},{6,4},{8,10},{10,8},{12,14},{14,12},{1,3},{3,1},... | collective-permute-start | bytes 1179656 | tf_op jit(solution)/shard_map/ppermute | solution.py:260
  9.7 24.9 %collective-permute-start = (bf16[12,128,128]{2,1,0:T(8,128)(2,1)S(1)}, bf16[12,128,128]{2,1,0:T(8,128)(2,1)S(1)}, u32[]{:S(2)}, u32[]{:S(2)}) collective-permute-start(bf16[12,128,128]{2,1,0:T(8,128)(2,1)S(1)} %copy-done), channel_id=1, source_target_pairs={{0,1},{1,0},{2,3},{3,2},{4,5},{5,4},{6,7},{7,6},{8,9},{9,8},{10,11... | collective-permute-start | bytes 1179656 | tf_op jit(solution)/shard_map/ppermute | solution.py:259
  24.2 10.3 %collective-permute-start.2 = (bf16[12,128,128]{2,1,0:T(8,128)(2,1)S(1)}, bf16[12,128,128]{2,1,0:T(8,128)(2,1)S(1)}, u32[]{:S(2)}, u32[]{:S(2)}) collective-permute-start(bf16[12,128,128]{2,1,0:T(8,128)(2,1)S(1)} %collective-permute-done.1.refs_3_), channel_id=1, source_target_pairs={{0,1},{1,0},{2,3},{3,2},{4,5},{5,4},{6,7},{7,6},{8,9},{9,8},{10,11... | collective-permute-start | bytes 1179656 | tf_op jit(solution)/shard_map/ppermute | solution.py:292
  30.6 24.0 %collective-permute-start.3 = (bf16[1,3,256,128]{3,2,1,0:T(8,128)(2,1)S(1)}, bf16[1,3,256,128]{3,2,1,0:T(8,128)(2,1)S(1)}, u32[]{:S(2)}, u32[]{:S(2)}) collective-permute-start(bf16[1,3,256,128]{3,2,1,0:T(8,128)(2,1)S(1)} %bitcast.11), channel_id=1, source_target_pairs={{0,12},{2,14},{4,8},{6,10},{8,4},{10,6},{12,0},{14,2},{1,13},{3,15... | collective-permute-start | bytes 589832 | tf_op jit(solution)/shard_map/ppermute | solution.py:290
  32.2 19.3 %collective-permute-start.4 = (bf16[1,3,256,128]{3,2,1,0:T(8,128)(2,1)S(1)}, bf16[1,3,256,128]{3,2,1,0:T(8,128)(2,1)S(1)}, u32[]{:S(2)}, u32[]{:S(2)}) collective-permute-start(bf16[1,3,256,128]{3,2,1,0:T(8,128)(2,1)S(1)} %bitcast.12), channel_id=1, source_target_pairs={{0,8},{2,10},{4,12},{6,14},{8,0},{10,2},{12,4},{14,6},{1,9},{3,11}... | collective-permute-start | bytes 589832 | tf_op jit(solution)/shard_map/ppermute | solution.py:290
  33.6 14.7 %collective-permute-start.5 = (bf16[1,3,256,128]{3,2,1,0:T(8,128)(2,1)S(1)}, bf16[1,3,256,128]{3,2,1,0:T(8,128)(2,1)S(1)}, u32[]{:S(2)}, u32[]{:S(2)}) collective-permute-start(bf16[1,3,256,128]{3,2,1,0:T(8,128)(2,1)S(1)} %bitcast.13), channel_id=1, source_target_pairs={{0,4},{2,6},{4,0},{6,2},{8,12},{10,14},{12,8},{14,10},{1,5},{3,7},... | collective-permute-start | bytes 589832 | tf_op jit(solution)/shard_map/ppermute | solution.py:290
  58.0 11.6 %collective-permute-start.8 = (f32[12,384]{1,0:T(8,128)S(1)}, f32[12,384]{1,0:T(8,128)S(1)}, u32[]{:S(2)}, u32[]{:S(2)}) collective-permute-start(f32[12,384]{1,0:T(8,128)S(1)} %get-tuple-element.12), channel_id=1, source_target_pairs={{0,3},{1,2},{2,1},{3,0},{4,7},{5,6},{6,5},{7,4},{8,11},{9,10},{10,... | collective-permute-start | bytes 55304 | tf_op jit(solution)/shard_map/ppermute | solution.py:312
  68.1 3.8 %collective-permute-start.7 = (f32[12,384]{1,0:T(8,128)S(1)}, f32[12,384]{1,0:T(8,128)S(1)}, u32[]{:S(2)}, u32[]{:S(2)}) collective-permute-start(f32[12,384]{1,0:T(8,128)S(1)} %get-tuple-element.12), channel_id=1, source_target_pairs={{0,2},{2,0},{4,6},{6,4},{8,10},{10,8},{12,14},{14,12},{1,3},{3,1},... | collective-permute-start | bytes 55304 | tf_op jit(solution)/shard_map/ppermute | solution.py:312
  68.1 3.8 %collective-permute-start.6 = (f32[12,384]{1,0:T(8,128)S(1)}, f32[12,384]{1,0:T(8,128)S(1)}, u32[]{:S(2)}, u32[]{:S(2)}) collective-permute-start(f32[12,384]{1,0:T(8,128)S(1)} %get-tuple-element.11), channel_id=1, source_target_pairs={{0,1},{1,0},{2,3},{3,2},{4,5},{5,4},{6,7},{7,6},{8,9},{9,8},{10,11... | collective-permute-start | bytes 55304 | tf_op jit(solution)/shard_map/ppermute | solution.py:311
